TPU v7x, 256 devices: a whole 4x4x8 slice. The times are simulated.
256 devices in a mesh: dp: 8 (over y, z_hi), tile: 32 (over x, z_lo, core).
Axes of the slice: x: 4, y: 4, z: 8 (z_hi: 2, z_lo: 4; z = z_hi * 4 + z_lo), core: 2. Of those that a mesh axis runs over, the one named last changes fastest.
Arguments:
- videos: bfloat16 [8, 32, 32, 64, 512], P('dp', 'tile'), may hold values from -6 to 6
- spatial_filter: bfloat16 [9, 512, 512], P(None, 'dp'), may hold values from -0.09375 to 0.09375
- temporal_filter: bfloat16 [3, 512, 512], P(None, 'dp'), may hold values from -0.15625 to 0.15625
- spatial_bias: float32 [512], replicated, may hold values from -3 to 3
- temporal_bias: float32 [512], replicated, may hold values from -3 to 3
Outputs:
- output: bfloat16 [8, 32, 32, 64, 512], P('dp', 'tile')
All inputs are finite; a program needn't handle non-finite values.
Results may differ from a plain program's by a relative error of at most 0.0044.
Values may be sent and summed in bfloat16 or wider, within the bound.
A program may use at most 128 MiB of HBM per device.

v0:
```python
import jax
import jax.numpy as jnp
from jax import lax
from jax.sharding import PartitionSpec as P


def padded_2(block, sides, width):
    for axis, dim in sides:
        count = lax.axis_size(axis)
        forward = [(i, i + 1) for i in range(count - 1)]
        backward = [(target, source) for source, target in forward]
        low = lax.ppermute(
            lax.slice_in_dim(block, block.shape[dim] - width, None, axis=dim), axis, forward
        )
        high = lax.ppermute(lax.slice_in_dim(block, 0, width, axis=dim), axis, backward)
        block = jnp.concatenate([low, block, high], axis=dim)
    return block


def spatial_term(padded, weight_piece):
    width = weight_piece.shape[1]
    height = padded.shape[2] - 2
    breadth = padded.shape[3] - 2
    columns = jnp.concatenate(
        [
            padded[:, :, row_off : row_off + height, col_off : col_off + breadth, :]
            for row_off in range(3)
            for col_off in range(3)
        ],
        axis=4,
    )
    matrix = weight_piece.reshape(9 * width, weight_piece.shape[2])
    return jnp.dot(columns.reshape(-1, 9 * width), matrix, preferred_element_type=jnp.float32)


def temporal_term(framed, weight_piece):
    width = weight_piece.shape[1]
    frames = framed.shape[1] - 2
    columns = jnp.concatenate([framed[:, lag : lag + frames] for lag in range(3)], axis=4)
    matrix = weight_piece.reshape(3 * width, weight_piece.shape[2])
    return jnp.dot(columns.reshape(-1, 3 * width), matrix, preferred_element_type=jnp.float32)


def per_device(videos, spatial_filter, temporal_filter, spatial_bias, temporal_bias):
    samples, frames, height, breadth, channels = videos.shape
    count_frames = videos.shape[1]
    padded = jnp.pad(videos, ((0, 0), (0, 0), (1, 1), (1, 1), (0, 0)))
    summed = spatial_term(padded, lax.all_gather(spatial_filter, "dp", axis=1, tiled=True))
    activated = jax.nn.silu(summed + spatial_bias).astype(jnp.bfloat16)
    hidden = activated.reshape(samples, count_frames, height, breadth, channels)
    framed = padded_2(hidden, (("tile", 1),), 1)
    result = temporal_term(framed, lax.all_gather(temporal_filter, "dp", axis=1, tiled=True))
    return (result + temporal_bias).astype(jnp.bfloat16).reshape(videos.shape)


def solution(mesh):
    return jax.shard_map(
        per_device,
        mesh=mesh,
        in_specs=(
            P("dp", "tile", None, None, None),
            P(None, "dp", None),
            P(None, "dp", None),
            P(),
            P(),
        ),
        out_specs=P("dp", "tile", None, None, None),
        check_vma=False,
    )
```

profile of v0, /device:TPU:34, one launch (start us, length us, event | category | flops | bytes accessed | tf_op | source)
XLA Modules:
  0.0 224.9 jit_solution(13520640981759495450)
XLA Ops:
  6.5 0.0 copy-start
  6.5 0.0 all-gather.3.cloned.1.call-start
  6.5 0.7 all-gather.3.cloned.1.call-update
  7.3 0.0 all-gather.5.cloned.1.call-start
  7.3 0.7 all-gather.5.cloned.1.call-update
  8.0 3.5 %slice_dynamic-update-slice_fusion.7 = bf16[1,1,32,64,4608]{4,3,2,1,0:T(8,128)(2,1)} fusion(bf16[1,1,32,64,512]{4,3,2,1,0:T(8,128)(2,1)} %param.5), kind=kLoop, calls=%fused_computation.15 | loop fusion | bytes 4194304
  11.5 0.0 copy-done
  11.5 1.6 slice_dynamic-update-slice_fusion.6
  13.1 2.5 %slice_dynamic-update-slice_fusion.5 = bf16[1,1,32,64,4608]{4,3,2,1,0:T(8,128)(2,1)} fusion(bf16[1,1,32,64,4608]{4,3,2,1,0:T(8,128)(2,1)} %slice_dynamic-update-slice_fusion.6, bf16[1,1,32,64,512]{4,3,2,1,0:T(8,128)(2,1)S(1)} %copy-done), kind=kLoop, calls=%fused_computation.13 | loop fusion | bytes 4194304
  15.7 2.7 %slice_dynamic-update-slice_fusion.4 = bf16[1,1,32,64,4608]{4,3,2,1,0:T(8,128)(2,1)} fusion(bf16[1,1,32,64,4608]{4,3,2,1,0:T(8,128)(2,1)} %slice_dynamic-update-slice_fusion.5, bf16[1,1,32,64,512]{4,3,2,1,0:T(8,128)(2,1)S(1)} %copy-done), kind=kLoop, calls=%fused_computation.12 | loop fusion | bytes 4194304
  18.4 1.6 constant_dynamic-update-slice_fusion
  20.0 2.5 %slice_dynamic-update-slice_fusion.3 = bf16[1,1,32,64,4608]{4,3,2,1,0:T(8,128)(2,1)} fusion(bf16[1,1,32,64,4608]{4,3,2,1,0:T(8,128)(2,1)} %constant_dynamic-update-slice_fusion, bf16[1,1,32,64,512]{4,3,2,1,0:T(8,128)(2,1)S(1)} %copy-done), kind=kLoop, calls=%fused_computation.11 | loop fusion | bytes 4194304
  22.5 2.7 %slice_dynamic-update-slice_fusion.2 = bf16[1,1,32,64,4608]{4,3,2,1,0:T(8,128)(2,1)} fusion(bf16[1,1,32,64,4608]{4,3,2,1,0:T(8,128)(2,1)} %slice_dynamic-update-slice_fusion.3, bf16[1,1,32,64,512]{4,3,2,1,0:T(8,128)(2,1)S(1)} %copy-done), kind=kLoop, calls=%fused_computation.10 | loop fusion | bytes 4194304
  25.2 0.0 copy-start.1
  25.2 1.6 slice_dynamic-update-slice_fusion.1
  26.9 2.6 %slice_dynamic-update-slice_fusion = bf16[1,1,32,64,4608]{4,3,2,1,0:T(8,128)(2,1)} fusion(bf16[1,1,32,64,4608]{4,3,2,1,0:T(8,128)(2,1)} %slice_dynamic-update-slice_fusion.1, bf16[1,1,32,64,512]{4,3,2,1,0:T(8,128)(2,1)S(1)} %copy-done), kind=kLoop, calls=%fused_computation.8 | loop fusion | bytes 4194304 | tf_op jit(solution)/shard_map/concatenate | solution.py:24
  29.4 97.0 %all-gather.3.cloned.1.call-done = bf16[9,512,512]{2,1,0:T(8,128)(2,1)} async-done(((bf16[9,64,512]{2,1,0:T(8,128)(2,1)}), bf16[9,512,512]{2,1,0:T(8,128)(2,1)}) %all-gather.3.cloned.1.call-update) | async-done | bytes 4718608 | tf_op jit(solution)/shard_map/all_gather | solution.py:48
  126.4 0.0 copy-done.1
  126.4 0.0 copy-start.2
  126.4 15.8 %multiply_convert_fusion = bf16[2048,512]{1,0:T(8,128)(2,1)S(1)} fusion(bf16[2048,4608]{1,0:T(8,128)(2,1)} %bitcast, bf16[4608,512]{1,0:T(8,128)(2,1)} %bitcast.10, f32[512]{0:T(512)S(1)} %copy-done.1), kind=kOutput, calls=%fused_computation.7 | convolution fusion | flops 9669967872 | bytes 25692160 | tf_op jit(solution)/shard_map/dot_general | solution.py:33
  142.2 1.9 collective-permute-start
  144.1 3.8 %collective-permute-start.1 = (bf16[1,1,32,64,512]{4,3,2,1,0:T(8,128)(2,1)S(1)}, bf16[1,1,32,64,512]{4,3,2,1,0:T(8,128)(2,1)}, u32[]{:S(2)}, u32[]{:S(2)}) collective-permute-start(bf16[1,1,32,64,512]{4,3,2,1,0:T(8,128)(2,1)S(1)} %bitcast.12), channel_id=1, source_target_pairs={{1,0},{2,1},{3,2},{4,3},{5,4},{6,5},{7,6},{8,7},{9,8},{10,9},{11,1... | collective-permute-start | bytes 6291464 | tf_op jit(solution)/shard_map/ppermute | solution.py:15
  148.0 54.9 %all-gather.5.cloned.1.call-done = bf16[3,512,512]{2,1,0:T(8,128)(2,1)} async-done(((bf16[3,64,512]{2,1,0:T(8,128)(2,1)}), bf16[3,512,512]{2,1,0:T(8,128)(2,1)}) %all-gather.5.cloned.1.call-update) | async-done | bytes 1572880 | tf_op jit(solution)/shard_map/all_gather | solution.py:52
  202.9 0.0 collective-permute-done
  202.9 7.7 %collective-permute-done.1 = bf16[1,1,32,64,512]{4,3,2,1,0:T(8,128)(2,1)} collective-permute-done((bf16[1,1,32,64,512]{4,3,2,1,0:T(8,128)(2,1)S(1)}, bf16[1,1,32,64,512]{4,3,2,1,0:T(8,128)(2,1)}, u32[]{:S(2)}, u32[]{:S(2)}) %collective-permute-start.1) | collective-permute-done | bytes 2097184 | tf_op jit(solution)/shard_map/ppermute | solution.py:15
  210.6 0.0 copy-done.2
  210.6 7.4 %add_convert_fusion = bf16[2048,512]{1,0:T(8,128)(2,1)} fusion(bf16[1536,512]{1,0:T(8,128)(2,1)} %bitcast.13, bf16[2048,512]{1,0:T(8,128)(2,1)} %bitcast.4, bf16[2048,512]{1,0:T(8,128)(2,1)S(1)} %multiply_convert_fusion, bf16[2048,512]{1,0:T(8,128)(2,1)} %bitcast.3, f32[512]{0:T(512)S(1)} %copy-done.2), kind=kOutput, calls=%fused_computation.6 | convolution fusion | flops 3242196992 | bytes 9963520 | tf_op jit(solution)/shard_map/dot_general | solution.py:41
Async XLA Ops:
  6.5 5.0 %copy-start = (bf16[1,1,32,64,512]{4,3,2,1,0:T(8,128)(2,1)S(1)}, bf16[1,1,32,64,512]{4,3,2,1,0:T(8,128)(2,1)}, u32[]{:S(2)}) copy-start(bf16[1,1,32,64,512]{4,3,2,1,0:T(8,128)(2,1)} %param.5) | copy-start | bytes 6291460
  6.5 119.9 %all-gather.3.cloned.1.call-start = ((), (), s32[]{:S(2)}) async-start(), calls=%async_computation | async-start | bytes 5308416 | tf_op jit(solution)/shard_map/all_gather | solution.py:48
  7.3 195.6 %all-gather.5.cloned.1.call-start = ((), (), s32[]{:S(2)}) async-start(), calls=%async_computation.1 | async-start | bytes 1769472 | tf_op jit(solution)/shard_map/all_gather | solution.py:52
  25.2 101.2 %copy-start.1 = (f32[512]{0:T(512)S(1)}, f32[512]{0:T(512)}, u32[]{:S(2)}) copy-start(f32[512]{0:T(512)} %param.8) | copy-start | bytes 6148
  126.4 84.2 %copy-start.2 = (f32[512]{0:T(512)S(1)}, f32[512]{0:T(512)}, u32[]{:S(2)}) copy-start(f32[512]{0:T(512)} %param.9) | copy-start | bytes 6148
  142.2 60.7 %collective-permute-start = (bf16[1,1,32,64,512]{4,3,2,1,0:T(8,128)(2,1)S(1)}, bf16[1,1,32,64,512]{4,3,2,1,0:T(8,128)(2,1)}, u32[]{:S(2)}, u32[]{:S(2)}) collective-permute-start(bf16[1,1,32,64,512]{4,3,2,1,0:T(8,128)(2,1)S(1)} %bitcast.11), channel_id=1, source_target_pairs={{0,1},{1,2},{2,3},{3,4},{4,5},{5,6},{6,7},{7,8},{8,9},{9,10},{10,1... | collective-permute-start | bytes 6291464 | tf_op jit(solution)/shard_map/ppermute | solution.py:12
  144.1 66.5 %collective-permute-start.1 = (bf16[1,1,32,64,512]{4,3,2,1,0:T(8,128)(2,1)S(1)}, bf16[1,1,32,64,512]{4,3,2,1,0:T(8,128)(2,1)}, u32[]{:S(2)}, u32[]{:S(2)}) collective-permute-start(bf16[1,1,32,64,512]{4,3,2,1,0:T(8,128)(2,1)S(1)} %bitcast.12), channel_id=1, source_target_pairs={{1,0},{2,1},{3,2},{4,3},{5,4},{6,5},{7,6},{8,7},{9,8},{10,9},{11,1... | collective-permute-start | bytes 6291464 | tf_op jit(solution)/shard_map/ppermute | solution.py:15
Sparse Core Ops, SparseCore 0:
  10.0 116.4 all-gather.2
  129.1 73.7 all-gather.4
where the time goes:
time: 228 us; the launch traced here: 225 us
  waiting for transfers between devices  161 us (71%)
  matrix products  23.2 us (10%)
  local copies, waits for them, and re-layouts  21.4 us (9%)
  between operations  13.4 us (6%)
  starting transfers between devices  5.79 us (3%)
    all_gather x1, waiting for transfers between devices, per_device(): lax.all_gather(spatial_filter, 'dp', axis=1, tiled=True)  97 us
    all_gather x1, waiting for transfers between devices, per_device(): lax.all_gather(temporal_filter, 'dp', axis=1, tiled=True)  54.9 us
    unnamed x14, local copies, waits for them, and re-layouts  18.9 us
    dot_general x1, matrix products, spatial_term(): jnp.dot(columns.reshape(-1, 9 * width), matrix, preferred_element_type=jn...  15.8 us
    ppermute x1, waiting for transfers between devices, padded_2(): lax.ppermute(lax.slice_in_dim(block, 0, width, axis=dim), axis, backward)  7.74 us
    dot_general x1, matrix products, temporal_term(): jnp.dot(columns.reshape(-1, 3 * width), matrix, preferred_element_type=jn...  7.43 us
  transfers between devices with their start and end apart: 4, of which 3 were waited for; matrix products, arithmetic and copies ran while one was open for 17% of the time, Pallas kernels for 0%

commit v1 on v0

v1 whole, which is shorter than its diff:
```python
import functools

import jax
import jax.numpy as jnp
from jax import lax
from jax.experimental import pallas as pl
from jax.experimental.pallas import tpu as pltpu
from jax.sharding import PartitionSpec as P

WIDTHS = (128, 128, 256)
ROWS = 256
TAPS_S, TAPS_T = 9, 3


def kernel(dims, vid_hbm, ws_hbm, wt_hbm, sb_ref, tb_ref, out_hbm, xcat, *rest):
    nb = len(WIDTHS)
    height, breadth, chans, shard = dims
    pixels = height * breadth
    chunks = pixels // ROWS
    wbuf = rest[:nb]
    wt = rest[nb]
    own = rest[nb + 1 : 2 * nb + 1]
    before = rest[2 * nb + 1 : 3 * nb + 1]
    after = rest[3 * nb + 1 : 4 * nb + 1]
    acc, outv, local_sem, wsend, wrecv, hsend, hrecv, osem = rest[4 * nb + 1 :]
    offs = [sum(WIDTHS[:b]) for b in range(nb)]
    half = shard // 2
    quarter = half // 2

    dp, t = lax.axis_index("dp"), lax.axis_index("tile")
    tiles = lax.axis_size("tile")
    y, zh = dp // 2, dp % 2
    core = t % 2
    zl = (t // 2) % 4
    partner = t + 1 - 2 * core
    y_up, y_dn, y_far = (y + 1) % 4, (y + 3) % 4, (y + 2) % 4
    up, dn = y_up * 2 + zh, y_dn * 2 + zh
    other = y * 2 + 1 - zh
    first, last = zl == 0, zl == 3
    edge = jnp.logical_or(first, last)
    base = t - zl * 2
    cross_tile = base + jnp.where(first, 6, 0)
    inward_tile = base + jnp.where(first, 2, 4)
    inward_back = base + jnp.where(zl == 1, 0, 6)
    has_before, has_after = t > 0, t < tiles - 1

    def remote(src, dst, ssem, rsem, to_dp, to_tile):
        return pltpu.make_async_remote_copy(
            src_ref=src, dst_ref=dst, send_sem=ssem, recv_sem=rsem,
            device_id={"dp": to_dp, "tile": to_tile}, device_id_type=pl.DeviceIdType.MESH,
        )

    vid_copy = pltpu.make_async_copy(
        vid_hbm, xcat.at[pl.ds(breadth, pixels), pl.ds(chans, chans)], local_sem.at[0]
    )
    groups = [(ws_hbm, wbuf[b], offs[b], WIDTHS[b]) for b in range(nb)] + [(wt_hbm, wt, 0, chans)]
    loads = []
    for g, (src, buf, off, width) in enumerate(groups):
        mine = pl.multiple_of(dp * shard, shard)
        loads.append(
            pltpu.make_async_copy(
                src.at[:, :, pl.ds(off, width)], buf.at[:, pl.ds(mine, shard), :], local_sem.at[1 + g]
            )
        )
    loads[0].start()
    vid_copy.start()
    for c in loads[1:]:
        c.start()

    barrier = pltpu.get_barrier_semaphore()

    def greet(to_dp, to_tile):
        pl.semaphore_signal(
            barrier, inc=1, device_id={"dp": to_dp, "tile": to_tile}, device_id_type=pl.DeviceIdType.MESH
        )

    greet(dp, partner)
    greet(up, t)
    greet(dn, t)

    @pl.when(edge)
    def _():
        greet(other, cross_tile)
        greet(dp, inward_tile)

    @pl.when(jnp.logical_not(edge))
    def _():
        greet(dp, inward_back)

    @pl.when(has_before)
    def _():
        greet(dp, t - 1)

    @pl.when(has_after)
    def _():
        greet(dp, t + 1)

    one = lambda flag: jnp.where(flag, 1, 0)
    pl.semaphore_wait(barrier, 4 + one(edge) + one(has_before) + one(has_after))

    def piece(g, shard_id, low, count):
        start = pl.multiple_of(shard_id * shard + low, quarter)
        return groups[g][1].at[:, pl.ds(start, count), :]

    def wcopy(g, slot, shard_id, low, count, to_dp, to_tile):
        ref = piece(g, shard_id, low, count)
        return remote(ref, ref, wsend.at[g, slot], wrecv.at[g, slot], to_dp, to_tile)

    my_low = core * half
    def far(y_at, zh_at):
        return y_at * 2 + zh_at

    def sends_y(g, first_slot, shard_id, dst_zh):
        wcopy(g, first_slot, shard_id, my_low, half, up, t).start()
        wcopy(g, first_slot + 1, shard_id, my_low, half, dn, t).start()

    def to_partner(g, k, shard_id):
        wcopy(g, 9 + k, shard_id, my_low, half, dp, partner).start()

    def stage_start(g):
        loads[g].wait()

        @pl.when(edge)
        def _():
            wcopy(g, 0, dp, my_low, half, other, cross_tile).start()

        sends_y(g, 1, dp, zh)

    def stage_z(g):
        wcopy(g, 0, other, my_low, half, dp, t).wait_recv()

        @pl.when(edge)
        def _():
            ref = piece(g, other, my_low, half)
            remote(ref, ref, wsend.at[g, 16], wrecv.at[g, 0], dp, inward_tile).start()

        sends_y(g, 3, other, 1 - zh)
        to_partner(g, 0, other)

    def stage_y(g, which):
        z_at = zh if which == 0 else 1 - zh
        slot = 1 + 2 * which
        from_dn, from_up = far(y_dn, z_at), far(y_up, z_at)
        wcopy(g, slot, from_dn, my_low, half, dp, t).wait_recv()
        wcopy(g, 5 + 2 * which, from_dn, my_low, quarter, up, t).start()
        to_partner(g, 1 + 2 * which, from_dn)
        wcopy(g, slot + 1, from_up, my_low, half, dp, t).wait_recv()
        wcopy(g, 6 + 2 * which, from_up, my_low + quarter, quarter, dn, t).start()
        to_partner(g, 2 + 2 * which, from_up)

    def stage_far(g):
        for which in range(2):
            shard_id = far(y_far, zh if which == 0 else 1 - zh)
            wcopy(g, 5 + 2 * which, shard_id, my_low, quarter, dp, t).wait_recv()
            wcopy(g, 6 + 2 * which, shard_id, my_low + quarter, quarter, dp, t).wait_recv()
            to_partner(g, 5 + which, shard_id)

    def partner_ids():
        return [
            other, far(y_dn, zh), far(y_up, zh), far(y_dn, 1 - zh), far(y_up, 1 - zh),
            far(y_far, zh), far(y_far, 1 - zh),
        ]

    def stage_done(g):
        for k, shard_id in enumerate(partner_ids()):
            wcopy(g, 9 + k, shard_id, (1 - core) * half, half, dp, t).wait_recv()

    def wait_sends(g):
        @pl.when(edge)
        def _():
            wcopy(g, 0, dp, my_low, half, other, cross_tile).wait_send()
            wcopy(g, 16, other, my_low, half, dp, inward_tile).wait_send()

        for slot in range(1, 5):
            wcopy(g, slot, dp, my_low, half, up, t).wait_send()
        for slot in range(5, 9):
            wcopy(g, slot, dp, my_low, quarter, up, t).wait_send()
        for k in range(7):
            wcopy(g, 9 + k, dp, my_low, half, dp, partner).wait_send()

    def hcopy(b, i, side):
        rows = pl.ds(pl.multiple_of(i * ROWS, ROWS), ROWS)
        slot = b * chunks + i
        if side == 0:
            return remote(own[b].at[rows], after[b].at[rows], hsend.at[0, slot], hrecv.at[0, slot], dp, t - 1)
        return remote(own[b].at[rows], before[b].at[rows], hsend.at[1, slot], hrecv.at[1, slot], dp, t + 1)

    def send_hidden(b, i):
        @pl.when(has_before)
        def _():
            hcopy(b, i, 0).start()

        @pl.when(has_after)
        def _():
            hcopy(b, i, 1).start()

    def spatial(b, i):
        width = WIDTHS[b]
        total = None
        for dy in range(3):
            start = pl.multiple_of(i * ROWS + dy * breadth, breadth)
            lhs = xcat[pl.ds(start, ROWS), :]
            rhs = wbuf[b][3 * dy : 3 * dy + 3].reshape(3 * chans, width)
            part = jnp.dot(lhs, rhs, preferred_element_type=jnp.float32)
            total = part if total is None else total + part
        total = total + sb_ref[:, offs[b] : offs[b] + width]
        hidden = total / (1.0 + jnp.exp(-total))
        own[b][pl.ds(pl.multiple_of(i * ROWS, ROWS), ROWS), :] = hidden.astype(jnp.bfloat16)

    stage_start(0)

    zeros = jnp.zeros((breadth, 3 * chans), jnp.bfloat16)
    xcat[0:breadth, :] = zeros
    xcat[breadth + pixels :, :] = zeros
    vid_copy.wait()

    @pl.loop(0, height)
    def _(r):
        rows = pl.ds(pl.multiple_of((r + 1) * breadth, breadth), breadth)
        line = xcat[rows, chans : 2 * chans].astype(jnp.float32)
        at = lax.broadcasted_iota(jnp.int32, (breadth, chans), 0)
        left = jnp.where(at == 0, 0.0, pltpu.roll(line, 1, 0))
        right = jnp.where(at == breadth - 1, 0.0, pltpu.roll(line, breadth - 1, 0))
        xcat[rows, 0:chans] = left.astype(jnp.bfloat16)
        xcat[rows, 2 * chans : 3 * chans] = right.astype(jnp.bfloat16)

    stage_z(0)
    stage_y(0, 0)
    stage_y(0, 1)
    stage_start(1)
    stage_far(0)
    stage_done(0)

    for b in range(nb):
        more = b + 1 <= nb

        @pl.loop(0, chunks)
        def _(i, b=b):
            spatial(b, i)

            @pl.when(i > 0)
            def _():
                send_hidden(b, i - 1)

            if b > 0:
                @pl.when(i == 0)
                def _():
                    send_hidden(b - 1, chunks - 1)

            g = b + 1

            @pl.when(i == chunks // 4 - 1)
            def _():
                stage_z(g)

            @pl.when(i == chunks // 2 - 1)
            def _():
                stage_y(g, 0)

            @pl.when(i == chunks // 2)
            def _():
                stage_y(g, 1)

            if g < nb:
                @pl.when(i == chunks // 2 + 1)
                def _():
                    stage_start(g + 1)

            @pl.when(i == chunks - 2)
            def _():
                stage_far(g)

        stage_done(b + 1)

    def temporal_own(i):
        rows = pl.ds(pl.multiple_of(i * ROWS, ROWS), ROWS)
        total = tb_ref[...]
        for b in range(nb):
            total = total + jnp.dot(
                own[b][rows, :], wt[1, offs[b] : offs[b] + WIDTHS[b], :], preferred_element_type=jnp.float32
            )
        acc[rows, :] = total

    temporal_own(0)
    send_hidden(nb - 1, chunks - 1)

    @pl.loop(1, chunks)
    def _(i):
        temporal_own(i)

    for b in range(nb):
        @pl.loop(0, chunks)
        def _(i, b=b):
            rows = pl.ds(pl.multiple_of(i * ROWS, ROWS), ROWS)
            span = slice(offs[b], offs[b] + WIDTHS[b])

            @pl.when(has_before)
            def _():
                hcopy(b, i, 1).wait_recv()
                acc[rows, :] += jnp.dot(before[b][rows, :], wt[0, span, :], preferred_element_type=jnp.float32)

            @pl.when(has_after)
            def _():
                hcopy(b, i, 0).wait_recv()
                acc[rows, :] += jnp.dot(after[b][rows, :], wt[2, span, :], preferred_element_type=jnp.float32)

            if b == nb - 1:
                outv[rows, :] = acc[rows, :].astype(jnp.bfloat16)
                pltpu.make_async_copy(outv.at[rows], out_hbm.at[rows], osem.at[i]).start()

    for g in range(nb + 1):
        wait_sends(g)

    @pl.loop(0, chunks)
    def _(i):
        for b in range(nb):
            @pl.when(has_before)
            def _():
                hcopy(b, i, 0).wait_send()

            @pl.when(has_after)
            def _():
                hcopy(b, i, 1).wait_send()

        rows = pl.ds(pl.multiple_of(i * ROWS, ROWS), ROWS)
        pltpu.make_async_copy(outv.at[rows], out_hbm.at[rows], osem.at[i]).wait()


def per_device(videos, spatial_filter, temporal_filter, spatial_bias, temporal_bias):
    _, _, height, breadth, chans = videos.shape
    shard = spatial_filter.shape[1]
    pixels = height * breadth
    nb = len(WIDTHS)
    chunks = pixels // ROWS
    bf = jnp.bfloat16
    hid = [pltpu.VMEM((pixels, w), bf) for w in WIDTHS]
    anywhere = pl.BlockSpec(memory_space=pl.ANY)
    vmem = pl.BlockSpec(memory_space=pltpu.VMEM)
    out = pl.pallas_call(
        functools.partial(kernel, (height, breadth, chans, shard)),
        out_shape=jax.ShapeDtypeStruct((pixels, chans), bf),
        in_specs=[anywhere, anywhere, anywhere, vmem, vmem],
        out_specs=anywhere,
        scratch_shapes=[
            pltpu.VMEM((pixels + 2 * breadth, 3 * chans), bf),
            *[pltpu.VMEM((TAPS_S, chans, w), bf) for w in WIDTHS],
            pltpu.VMEM((TAPS_T, chans, chans), bf),
            *hid, *hid, *hid,
            pltpu.VMEM((pixels, chans), jnp.float32),
            pltpu.VMEM((pixels, chans), bf),
            pltpu.SemaphoreType.DMA((nb + 2,)),
            pltpu.SemaphoreType.DMA((nb + 1, 17)),
            pltpu.SemaphoreType.DMA((nb + 1, 17)),
            pltpu.SemaphoreType.DMA((2, nb * chunks)),
            pltpu.SemaphoreType.DMA((2, nb * chunks)),
            pltpu.SemaphoreType.DMA((chunks,)),
        ],
        compiler_params=pltpu.CompilerParams(
            collective_id=0, has_side_effects=True, vmem_limit_bytes=56 * 1024 * 1024
        ),
    )(
        videos.reshape(pixels, chans),
        spatial_filter,
        temporal_filter,
        spatial_bias.reshape(1, chans),
        temporal_bias.reshape(1, chans),
    )
    return out.reshape(videos.shape)


def solution(mesh):
    return jax.shard_map(
        per_device,
        mesh=mesh,
        in_specs=(
            P("dp", "tile", None, None, None),
            P(None, "dp", None),
            P(None, "dp", None),
            P(),
            P(),
        ),
        out_specs=P("dp", "tile", None, None, None),
        check_vma=False,
    )
```

time: 228 us -> 84.6 us (0.37)
  waiting for transfers between devices: 161 us -> 0 us
  Pallas kernels: 0 us -> 80.1 us
  matrix products: 23.2 us -> 0 us
  local copies, waits for them, and re-layouts: 21.4 us -> 3.13 us
  between operations: 13.4 us -> 0.01 us
  starting transfers between devices: 5.79 us -> 0 us
    all_gather x2 -> x0, waiting for transfers between devices: 152 us -> none  [the longest x1 97 us: per_device(): lax.all_gather(spatial_filter, 'dp', axis=1, tiled=True)]
    pallas_call x0 -> x1, Pallas kernels: none -> 80.1 us  [per_device(): pl.pallas_call(functools.partial(kernel, (height, breadth, chans, shard))...]
    dot_general x2 -> x0, matrix products: 23.2 us -> none  [the longest x1 15.8 us: spatial_term(): jnp.dot(columns.reshape(-1, 9 * width), matrix, preferred_element_type=jn...]
    unnamed x14 -> x1, local copies, waits for them, and re-layouts: 18.9 us -> 3.13 us
    ppermute x2 -> x0, waiting for transfers between devices: 7.74 us -> none  [the longest x1 7.74 us: padded_2(): lax.ppermute(lax.slice_in_dim(block, 0, width, axis=dim), axis, backward)]
    ppermute x2 -> x0, starting transfers between devices: 5.75 us -> none  [the longest x1 3.82 us: padded_2(): lax.ppermute(lax.slice_in_dim(block, 0, width, axis=dim), axis, backward)]
    concatenate x1 -> x0, local copies, waits for them, and re-layouts: 2.58 us -> none  [spatial_term(): jnp.concatenate([padded[:, :, row_off:row_off + height, col_off:col_off +...]
  transfers between devices with their start and end apart: 4 -> 0, of which waited for: 3 -> 0; matrix products, arithmetic and copies ran while one was open for 17% -> 0% of each run, Pallas kernels for 0% -> 0%
where the time goes in v1:
time: 84.6 us; the launch traced here: 83.2 us
  Pallas kernels  80.1 us (95%)
  local copies, waits for them, and re-layouts  3.13 us (4%)
    pallas_call x1, Pallas kernels, per_device(): pl.pallas_call(functools.partial(kernel, (height, breadth, chans, shard))...  80.1 us
    unnamed x1, local copies, waits for them, and re-layouts  3.13 us

profile of v1, /device:TPU:34, one launch (start us, length us, event | category | flops | bytes accessed | tf_op | source)
XLA Modules:
  0.0 83.2 jit_solution(6599003039261301660)
XLA Ops:
  0.0 80.1 %shard_map.55 = bf16[2048,512]{1,0:T(8,128)(2,1)} custom-call(bf16[2048,512]{1,0:T(8,128)(2,1)} %bitcast.5, bf16[9,64,512]{2,1,0:T(8,128)(2,1)} %ws_hbm.1, bf16[3,64,512]{2,1,0:T(8,128)(2,1)} %wt_hbm.1, f32[1,512]{1,0:T(1,128)} %bitcast.6, f32[1,512]{1,0:T(1,128)} %bitcast.7), custom_call_target="tpu_custom_call" | custom-call | tf_op jit(solution)/shard_map/pallas_call | solution.py:339
  80.1 3.1 %copy.7 = bf16[1,1,32,64,512]{4,3,2,1,0:T(8,128)(2,1)} copy(bf16[1,1,32,64,512]{4,3,2,1,0:T(8,128)(2,1)} %bitcast.4) | data formatting | bytes 4194304

commit v2 on v0

v2 whole, which is shorter than its diff:
```python
import functools

import jax
import jax.numpy as jnp
from jax import lax
from jax.experimental import pallas as pl
from jax.experimental.pallas import tpu as pltpu
from jax.sharding import PartitionSpec as P

BLOCK = 128
ROWS = 512
TAPS_S, TAPS_T = 9, 3
MESH = pl.DeviceIdType.MESH


def kernel(
    dims, vid_hbm, ws_hbm, wt_hbm, sb_ref, tb_ref, out_hbm,
    xcat, wb, wt, own, before, after, acc, outv,
    local_sem, wsend, wrecv, xsend, xrecv, psend, precv, hsend, hrecv, osem,
):
    height, breadth, chans, shard = dims
    pixels = height * breadth
    chunks = pixels // ROWS
    blocks = chans // BLOCK
    half = shard // 2

    dp, t = lax.axis_index("dp"), lax.axis_index("tile")
    tiles = lax.axis_size("tile")
    y, zh = dp // 2, dp % 2
    core, zl, x = t % 2, (t // 2) % 4, t // 8
    partner = t + 1 - 2 * core
    up, dn = ((y + 1) % 4) * 2 + zh, ((y + 3) % 4) * 2 + zh
    other = y * 2 + 1 - zh
    first, last = zl == 0, zl == 3
    edge = jnp.logical_or(first, last)
    base = t - zl * 2
    cross_tile = base + jnp.where(first, 6, 0)
    inward_tile = base + jnp.where(first, 2, 4)
    inward_back = base + jnp.where(zl == 1, 0, 6)
    x_next, x_prev = (t + 8) % tiles, (t + tiles - 8) % tiles
    has_before, has_after = t > 0, t < tiles - 1
    is_one = core == 1
    is_zero = core == 0

    block_a, block_b, block_c, block_d = x, (x + 2) % 4, (x + 1) % 4, (x + 3) % 4
    carried = jnp.where(is_zero, zh, 1 - zh)

    def shard_of(k, z_at):
        return ((y + k) % 4) * 2 + z_at

    def remote(src, dst, ssem, rsem, to_dp, to_tile):
        return pltpu.make_async_remote_copy(
            src_ref=src, dst_ref=dst, send_sem=ssem, recv_sem=rsem,
            device_id={"dp": to_dp, "tile": to_tile}, device_id_type=MESH,
        )

    mine = pl.ds(pl.multiple_of(dp * shard, shard), shard)

    def columns(j):
        return pl.ds(pl.multiple_of(j * BLOCK, BLOCK), BLOCK)

    def load_block(n, j):
        return pltpu.make_async_copy(ws_hbm.at[:, :, columns(j)], wb.at[j, :, mine, :], local_sem.at[n])

    vid_copy = pltpu.make_async_copy(
        vid_hbm, xcat.at[pl.ds(breadth, pixels), pl.ds(chans, chans)], local_sem.at[5]
    )
    loads = [load_block(n, j) for n, j in enumerate((block_a, block_b, block_c, block_d))]
    loads.append(pltpu.make_async_copy(wt_hbm, wt.at[:, mine, :], local_sem.at[4]))
    for n in (0, 1, 4):
        loads[n].start()
    vid_copy.start()
    for n in (2, 3):
        loads[n].start()

    barrier = pltpu.get_barrier_semaphore()

    def greet(to_dp, to_tile):
        pl.semaphore_signal(barrier, inc=1, device_id={"dp": to_dp, "tile": to_tile}, device_id_type=MESH)

    greet(dp, partner)
    greet(up, t)
    greet(dn, t)
    greet(dp, x_next)
    greet(dp, x_prev)

    @pl.when(edge)
    def _():
        greet(other, cross_tile)
        greet(dp, inward_tile)

    @pl.when(jnp.logical_not(edge))
    def _():
        greet(dp, inward_back)

    @pl.when(has_before)
    def _():
        greet(dp, t - 1)

    @pl.when(has_after)
    def _():
        greet(dp, t + 1)

    one = lambda flag: jnp.where(flag, 1, 0)
    pl.semaphore_wait(barrier, 6 + one(edge) + one(has_before) + one(has_after))

    bufs = [wb.at[block_a], wb.at[block_b], wt]

    def piece(g, shard_id, low=0, count=None):
        count = shard if count is None else count
        start = pl.multiple_of(shard_id * shard + low, half)
        return bufs[g].at[:, pl.ds(start, count), :]

    def ring(g, send, recv, shard_id, to_dp, to_tile, low=0, count=None):
        ref = piece(g, shard_id, low, count)
        return remote(ref, ref, wsend.at[g, send], wrecv.at[g, recv], to_dp, to_tile)

    def from_x(n, k, shard_id, to_tile):
        ref = wb.at[block_a, :, pl.ds(pl.multiple_of(shard_id * shard, shard), shard), :]
        return remote(ref, ref, xsend.at[n, k], xrecv.at[n, k], dp, to_tile)

    def spread(g, k):
        shard_id = shard_of(k, carried)
        ring(g, 6 + k, 5 + k, shard_id, dp, partner).start()
        if g == 0:
            from_x(0, k, shard_id, x_next).start()
            from_x(1, k, shard_id, x_prev).start()

    def start_z(g):
        @pl.when(jnp.logical_and(is_one, edge))
        def _():
            ring(g, 0, 0, dp, other, cross_tile).start()

    def start_y(g):
        shard_id = shard_of(0, carried)
        ring(g, 2, 1, shard_id, up, t).start()
        ring(g, 3, 2, shard_id, dn, t).start()

    def stage_z(g):
        @pl.when(is_one)
        def _():
            ring(g, 0, 0, other, dp, t).wait_recv()
            start_y(g)

            @pl.when(edge)
            def _():
                ring(g, 1, 0, other, dp, inward_tile).start()

            spread(g, 0)

    def stage_y(g):
        from_dn, from_up = shard_of(3, carried), shard_of(1, carried)
        ring(g, 2, 1, from_dn, up, t).wait_recv()
        ring(g, 4, 3, from_dn, up, t, 0, half).start()
        ring(g, 3, 2, from_up, dn, t).wait_recv()
        ring(g, 5, 4, from_up, dn, t, half, half).start()
        spread(g, 3)
        spread(g, 1)

    def stage_far(g):
        far = shard_of(2, carried)
        ring(g, 4, 3, far, up, t, 0, half).wait_recv()
        ring(g, 5, 4, far, dn, t, half, half).wait_recv()
        spread(g, 2)

    def stage_done(g):
        for k in range(4):
            wait = ring(g, 6 + k, 5 + k, shard_of(k, 1 - carried), dp, partner).wait_recv
            if k == 0:
                pl.when(is_zero)(wait)
            else:
                wait()

    def x_piece(n, k, shard_id):
        block = block_d if n == 0 else block_c
        ref = wb.at[block, :, pl.ds(pl.multiple_of(shard_id * shard, shard), shard), :]
        arrived = remote(ref, ref, xsend.at[n, k], xrecv.at[n, k], dp, x_next)
        onward = remote(ref, ref, psend.at[n, k], precv.at[n, k], dp, partner)
        return arrived, onward

    def stage_x(k):
        def run():
            for n in range(2):
                arrived, onward = x_piece(n, k, shard_of(k, carried))
                arrived.wait_recv()
                onward.start()

        if k == 0:
            pl.when(is_one)(run)
        else:
            run()

    def stage_x_done():
        for k in range(4):
            def run():
                for n in range(2):
                    x_piece(n, k, shard_of(k, 1 - carried))[1].wait_recv()

            if k == 0:
                pl.when(is_zero)(run)
            else:
                run()

    def wait_sends():
        for g in range(3):
            @pl.when(jnp.logical_and(is_one, edge))
            def _():
                ring(g, 0, 0, dp, other, cross_tile).wait_send()
                ring(g, 1, 0, dp, dp, inward_tile).wait_send()

            for slot in (2, 3):
                ring(g, slot, 0, dp, up, t).wait_send()
            for slot in (4, 5):
                ring(g, slot, 0, dp, up, t, 0, half).wait_send()
            for k in range(4):
                def run():
                    ring(g, 6 + k, 5 + k, dp, dp, partner).wait_send()
                    if g == 0:
                        for n in range(2):
                            from_x(n, k, dp, x_next).wait_send()
                            x_piece(n, k, dp)[1].wait_send()

                if k == 0:
                    pl.when(is_one)(run)
                else:
                    run()

    def rows_of(i):
        return pl.ds(pl.multiple_of(i * ROWS, ROWS), ROWS)

    def hcopy(j, i, side):
        slot = j * chunks + i
        src = own.at[j, rows_of(i), :]
        if side == 0:
            return remote(src, after.at[j, rows_of(i), :], hsend.at[0, slot], hrecv.at[0, slot], dp, t - 1)
        return remote(src, before.at[j, rows_of(i), :], hsend.at[1, slot], hrecv.at[1, slot], dp, t + 1)

    def send_hidden(pair, i):
        for j in pair:
            @pl.when(has_before)
            def _():
                hcopy(j, i, 0).start()

            @pl.when(has_after)
            def _():
                hcopy(j, i, 1).start()

    def spatial(pair, i):
        total = None
        for dy in range(3):
            start = pl.multiple_of(i * ROWS + dy * breadth, breadth)
            lhs = xcat[pl.ds(start, ROWS), :]
            rhs = jnp.concatenate(
                [wb[j, 3 * dy : 3 * dy + 3].reshape(3 * chans, BLOCK) for j in pair], axis=1
            )
            part = jnp.dot(lhs, rhs, preferred_element_type=jnp.float32)
            total = part if total is None else total + part
        total = total + jnp.concatenate([sb_ref[j] for j in pair], axis=1)
        hidden = (total / (1.0 + jnp.exp(-total))).astype(jnp.bfloat16)
        for n, j in enumerate(pair):
            own[j, rows_of(i), :] = hidden[:, n * BLOCK : (n + 1) * BLOCK]

    start_z_all = lambda: [start_z(g) for g in range(3)]
    loads[0].wait()
    start_z(0)
    pl.when(is_zero)(lambda: start_y(0))
    loads[1].wait()
    start_z(1)
    pl.when(is_zero)(lambda: start_y(1))
    loads[4].wait()
    start_z(2)

    zeros = jnp.zeros((breadth, 3 * chans), jnp.bfloat16)
    xcat[0:breadth, :] = zeros
    xcat[breadth + pixels :, :] = zeros
    vid_copy.wait()

    @pl.loop(0, height)
    def _(r):
        rows = pl.ds(pl.multiple_of((r + 1) * breadth, breadth), breadth)
        line = xcat[rows, chans : 2 * chans].astype(jnp.float32)
        at = lax.broadcasted_iota(jnp.int32, (breadth, chans), 0)
        left = jnp.where(at == 0, 0.0, pltpu.roll(line, 1, 0))
        right = jnp.where(at == breadth - 1, 0.0, pltpu.roll(line, breadth - 1, 0))
        xcat[rows, 0:chans] = left.astype(jnp.bfloat16)
        xcat[rows, 2 * chans : 3 * chans] = right.astype(jnp.bfloat16)

    stage_z(0)
    stage_y(0)
    stage_z(1)
    stage_far(0)
    stage_y(1)
    stage_far(1)
    pl.when(is_zero)(lambda: start_y(2))
    stage_done(0)
    stage_done(1)
    loads[2].wait()
    loads[3].wait()

    pair_0, pair_1 = (block_a, block_b), (block_c, block_d)

    @pl.loop(0, chunks)
    def _(i):
        spatial(pair_0, i)

        @pl.when(i > 0)
        def _():
            send_hidden(pair_0, i - 1)

        @pl.when(i == 0)
        def _():
            stage_x(0)
            stage_x(3)
            stage_x(1)

        @pl.when(i == 1)
        def _():
            stage_z(2)
            stage_x(2)

        @pl.when(i == 2)
        def _():
            stage_y(2)

    stage_x_done()

    @pl.loop(0, chunks)
    def _(i):
        spatial(pair_1, i)

        @pl.when(i == 0)
        def _():
            send_hidden(pair_0, chunks - 1)
            stage_far(2)

        @pl.when(i > 0)
        def _():
            send_hidden(pair_1, i - 1)

    stage_done(2)

    def taps(lag, j):
        return wt[lag, pl.ds(pl.multiple_of(j * BLOCK, BLOCK), BLOCK), :]

    def temporal(lag, src, pair, i):
        lhs = jnp.concatenate([src[j, rows_of(i), :] for j in pair], axis=1)
        rhs = jnp.concatenate([taps(lag, j) for j in pair], axis=0)
        return jnp.dot(lhs, rhs, preferred_element_type=jnp.float32)

    def temporal_own(i):
        acc[rows_of(i), :] = temporal(1, own, pair_0, i) + temporal(1, own, pair_1, i) + tb_ref[...]

    temporal_own(0)
    send_hidden(pair_1, chunks - 1)

    @pl.loop(1, chunks)
    def _(i):
        temporal_own(i)

    x_before, x_after = (t + tiles - 1) % tiles // 8, (t + 1) % tiles // 8
    for p in range(2):
        @pl.loop(0, chunks)
        def _(i, p=p):
            rows = rows_of(i)

            @pl.when(has_before)
            def _():
                pair = ((x_before + p) % 4, (x_before + p + 2) % 4)
                for j in pair:
                    hcopy(j, i, 1).wait_recv()
                acc[rows, :] += temporal(0, before, pair, i)

            @pl.when(has_after)
            def _():
                pair = ((x_after + p) % 4, (x_after + p + 2) % 4)
                for j in pair:
                    hcopy(j, i, 0).wait_recv()
                acc[rows, :] += temporal(2, after, pair, i)

            if p == 1:
                outv[rows, :] = acc[rows, :].astype(jnp.bfloat16)
                pltpu.make_async_copy(outv.at[rows], out_hbm.at[rows], osem.at[i]).start()

    wait_sends()

    @pl.loop(0, chunks)
    def _(i):
        for j in range(blocks):
            @pl.when(has_before)
            def _():
                hcopy(j, i, 0).wait_send()

            @pl.when(has_after)
            def _():
                hcopy(j, i, 1).wait_send()

        pltpu.make_async_copy(outv.at[rows_of(i)], out_hbm.at[rows_of(i)], osem.at[i]).wait()


def per_device(videos, spatial_filter, temporal_filter, spatial_bias, temporal_bias):
    _, _, height, breadth, chans = videos.shape
    shard = spatial_filter.shape[1]
    pixels = height * breadth
    blocks = chans // BLOCK
    chunks = pixels // ROWS
    bf = jnp.bfloat16
    anywhere = pl.BlockSpec(memory_space=pl.ANY)
    vmem = pl.BlockSpec(memory_space=pltpu.VMEM)
    dma = pltpu.SemaphoreType.DMA
    out = pl.pallas_call(
        functools.partial(kernel, (height, breadth, chans, shard)),
        out_shape=jax.ShapeDtypeStruct((pixels, chans), bf),
        in_specs=[anywhere, anywhere, anywhere, vmem, vmem],
        out_specs=anywhere,
        scratch_shapes=[
            pltpu.VMEM((pixels + 2 * breadth, 3 * chans), bf),
            pltpu.VMEM((blocks, TAPS_S, chans, BLOCK), bf),
            pltpu.VMEM((TAPS_T, chans, chans), bf),
            pltpu.VMEM((blocks, pixels, BLOCK), bf),
            pltpu.VMEM((blocks, pixels, BLOCK), bf),
            pltpu.VMEM((blocks, pixels, BLOCK), bf),
            pltpu.VMEM((pixels, chans), jnp.float32),
            pltpu.VMEM((pixels, chans), bf),
            dma((6,)),
            dma((3, 10)), dma((3, 9)),
            dma((2, 4)), dma((2, 4)),
            dma((2, 4)), dma((2, 4)),
            dma((2, blocks * chunks)), dma((2, blocks * chunks)),
            dma((chunks,)),
        ],
        compiler_params=pltpu.CompilerParams(
            collective_id=0, has_side_effects=True, vmem_limit_bytes=56 * 1024 * 1024
        ),
    )(
        videos.reshape(pixels, chans),
        spatial_filter,
        temporal_filter,
        spatial_bias.reshape(blocks, 1, BLOCK),
        temporal_bias.reshape(1, chans),
    )
    return out.reshape(videos.shape)


def solution(mesh):
    return jax.shard_map(
        per_device,
        mesh=mesh,
        in_specs=(
            P("dp", "tile", None, None, None),
            P(None, "dp", None),
            P(None, "dp", None),
            P(),
            P(),
        ),
        out_specs=P("dp", "tile", None, None, None),
        check_vma=False,
    )
```

time: 228 us -> 84.6 us (0.37)
  the two profiles are of different devices: /device:TPU:34 before, /device:TPU:6 now
where the time goes in v2:
time: 84.6 us; the launch traced here: 84.4 us
  Pallas kernels  81.3 us (96%)
  local copies, waits for them, and re-layouts  3.13 us (4%)
    pallas_call x1, Pallas kernels, per_device(): pl.pallas_call(functools.partial(kernel, (height, breadth, chans, shard))...  81.3 us
    unnamed x1, local copies, waits for them, and re-layouts  3.13 us

profile of v2, /device:TPU:6, one launch (start us, length us, event | category | flops | bytes accessed | tf_op | source)
XLA Modules:
  0.0 84.4 jit_solution(2094612950388706189)
XLA Ops:
  0.0 81.3 %shard_map.55 = bf16[2048,512]{1,0:T(8,128)(2,1)} custom-call(bf16[2048,512]{1,0:T(8,128)(2,1)} %bitcast.5, bf16[9,64,512]{2,1,0:T(8,128)(2,1)} %ws_hbm.1, bf16[3,64,512]{2,1,0:T(8,128)(2,1)} %wt_hbm.1, f32[4,1,128]{2,1,0:T(1,128)} %bitcast.6, f32[1,512]{1,0:T(1,128)} %bitcast.7), custom_call_target="tpu_custom_call" | custom-call | tf_op jit(solution)/shard_map/pallas_call | solution.py:410
  81.3 3.1 %copy.7 = bf16[1,1,32,64,512]{4,3,2,1,0:T(8,128)(2,1)} copy(bf16[1,1,32,64,512]{4,3,2,1,0:T(8,128)(2,1)} %bitcast.4) | data formatting | bytes 4194304

commit v3 on v2

v3 whole, which is shorter than its diff:
```python
import functools

import jax
import jax.numpy as jnp
from jax import lax
from jax.experimental import pallas as pl
from jax.experimental.pallas import tpu as pltpu
from jax.sharding import PartitionSpec as P

BLOCK = 128
ROWS = 512
FAR_CHUNKS = 3
TAPS_S, TAPS_T = 9, 3
MESH = pl.DeviceIdType.MESH


def kernel(
    dims, vid_hbm, ws_hbm, wt_hbm, sb_ref, tb_ref, out_hbm,
    xcat, xcat_far, vid_far, wb, wt, own, near, acc, outv,
    local_sem, wsend, wrecv, xsend, xrecv, psend, precv, hsend, hrecv, vsem, osem,
):
    height, breadth, chans, shard = dims
    pixels = height * breadth
    chunks = pixels // ROWS
    blocks = chans // BLOCK
    group = chans // 2
    half = shard // 2

    dp, t = lax.axis_index("dp"), lax.axis_index("tile")
    tiles = lax.axis_size("tile")
    y, zh = dp // 2, dp % 2
    core, zl, x = t % 2, (t // 2) % 4, t // 8
    partner = t + 1 - 2 * core
    up, dn = ((y + 1) % 4) * 2 + zh, ((y + 3) % 4) * 2 + zh
    other = y * 2 + 1 - zh
    first, last = zl == 0, zl == 3
    edge = jnp.logical_or(first, last)
    base = t - zl * 2
    cross_edge = base + jnp.where(first, 6, 0)
    cross_inner = base + jnp.where(first, 4, 2)
    inner_source = base + jnp.where(zl == 1, 6, 0)
    x_next, x_prev = (t + 8) % tiles, (t + tiles - 8) % tiles
    has_before, has_after = t > 0, t < tiles - 1
    far_before = jnp.logical_and(t % 8 == 0, has_before)
    far_after = jnp.logical_and(t % 8 == 7, has_after)
    far_any = jnp.logical_or(far_before, far_after)
    far_side = jnp.where(far_after, 1, 0)
    far_tile = jnp.where(far_after, t + 1, t - 1)
    is_one = core == 1
    is_zero = core == 0

    block_a, block_b, block_c, block_d = x, (x + 2) % 4, (x + 1) % 4, (x + 3) % 4
    carried = jnp.where(is_zero, zh, 1 - zh)

    def remote(src, dst, ssem, rsem, to_dp, to_tile):
        return pltpu.make_async_remote_copy(
            src_ref=src, dst_ref=dst, send_sem=ssem, recv_sem=rsem,
            device_id={"dp": to_dp, "tile": to_tile}, device_id_type=MESH,
        )

    def columns(j):
        return pl.ds(pl.multiple_of(j * BLOCK, BLOCK), BLOCK)

    def block_piece(j, y_at, z_at, low=0, count=None):
        count = shard if count is None else count
        return wb.at[j, z_at, :, pl.ds(pl.multiple_of(y_at * shard + low, half), count), :]

    def piece(g, y_at, z_at, low=0, count=None):
        if g < 2:
            return block_piece((block_a, block_b)[g], y_at, z_at, low, count)
        count = shard if count is None else count
        return wt.at[:, pl.ds(pl.multiple_of((y_at * 2 + z_at) * shard + low, half), count), :]

    def source(g):
        return wt_hbm if g == 2 else ws_hbm.at[:, :, columns((block_a, block_b)[g])]

    vid_copy = pltpu.make_async_copy(vid_hbm, outv, local_sem.at[5])
    loads = [
        pltpu.make_async_copy(ws_hbm.at[:, :, columns(j)], block_piece(j, y, zh), local_sem.at[n])
        for n, j in enumerate((block_a, block_b, block_c, block_d))
    ]
    loads.append(pltpu.make_async_copy(wt_hbm, piece(2, y, zh), local_sem.at[4]))
    vid_copy.start()
    for load in loads:
        load.start()

    barrier = pltpu.get_barrier_semaphore()

    def greet(to_dp, to_tile):
        pl.semaphore_signal(barrier, inc=1, device_id={"dp": to_dp, "tile": to_tile}, device_id_type=MESH)

    greet(dp, partner)
    greet(up, t)
    greet(dn, t)
    greet(dp, x_next)
    greet(dp, x_prev)

    @pl.when(edge)
    def _():
        greet(other, cross_edge)
        greet(other, cross_inner)

    @pl.when(jnp.logical_not(edge))
    def _():
        greet(other, inner_source)

    @pl.when(has_before)
    def _():
        greet(dp, t - 1)

    @pl.when(has_after)
    def _():
        greet(dp, t + 1)

    one = lambda flag: jnp.where(flag, 1, 0)
    pl.semaphore_wait(barrier, 6 + one(edge) + one(has_before) + one(has_after))

    def ring(g, send, recv, y_at, z_at, to_dp, to_tile, low=0, count=None, src=None):
        ref = piece(g, y_at, z_at, low, count)
        return remote(ref if src is None else src, ref, wsend.at[g, send], wrecv.at[g, recv], to_dp, to_tile)

    def from_x(n, k, y_at, to_tile):
        ref = block_piece(block_a, y_at, carried)
        return remote(ref, ref, xsend.at[n, k], xrecv.at[n, k], dp, to_tile)

    def y_of(k):
        return (y + k) % 4

    def spread(g, k):
        ring(g, 6 + k, 5 + k, y_of(k), carried, dp, partner).start()
        if g == 0:
            from_x(0, k, y_of(k), x_next).start()
            from_x(1, k, y_of(k), x_prev).start()

    def start_z(g):
        ring(g, 1, 0, y, zh, other, cross_inner, src=source(g)).start()
        ring(g, 0, 0, y, zh, other, cross_edge, src=source(g)).start()

    def start_y(g, src=None):
        ring(g, 2, 1, y, carried, up, t, src=src).start()
        ring(g, 3, 2, y, carried, dn, t, src=src).start()

    def stage_z(g):
        ring(g, 0, 0, y, 1 - zh, dp, partner).wait_recv()
        start_y(g)
        spread(g, 0)

    def stage_y(g):
        ring(g, 2, 1, y_of(3), carried, up, t).wait_recv()
        ring(g, 4, 3, y_of(3), carried, up, t, 0, half).start()
        ring(g, 3, 2, y_of(1), carried, dn, t).wait_recv()
        ring(g, 5, 4, y_of(1), carried, dn, t, half, half).start()
        spread(g, 3)
        spread(g, 1)

    def stage_far(g):
        ring(g, 4, 3, y_of(2), carried, up, t, 0, half).wait_recv()
        ring(g, 5, 4, y_of(2), carried, dn, t, half, half).wait_recv()
        spread(g, 2)

    def stage_done(g, ks):
        for k in ks:
            ring(g, 6 + k, 5 + k, y_of(k), 1 - carried, dp, partner).wait_recv()

    def onward(n, k, z_at):
        ref = block_piece((block_d, block_c)[n], y_of(k), z_at)
        return remote(ref, ref, psend.at[n, k], precv.at[n, k], dp, partner)

    def stage_x(k):
        for n in range(2):
            ref = block_piece((block_d, block_c)[n], y_of(k), carried)
            remote(ref, ref, xsend.at[n, k], xrecv.at[n, k], dp, x_next).wait_recv()
            onward(n, k, carried).start()

    def stage_x_done(ks):
        for k in ks:
            for n in range(2):
                onward(n, k, 1 - carried).wait_recv()

    def wait_sends():
        for g in range(3):
            @pl.when(jnp.logical_and(is_one, edge))
            def _():
                ring(g, 0, 0, y, zh, other, cross_edge).wait_send()
                ring(g, 1, 0, y, zh, other, cross_inner).wait_send()

            for slot in (2, 3):
                ring(g, slot, 0, y, carried, up, t).wait_send()
            for slot in (4, 5):
                ring(g, slot, 0, y, carried, up, t, 0, half).wait_send()
            for k in range(4):
                def run():
                    ring(g, 6 + k, 5 + k, y, carried, dp, partner).wait_send()
                    if g == 0:
                        for n in range(2):
                            from_x(n, k, y, x_next).wait_send()
                            onward(n, k, carried).wait_send()

                if k == 0:
                    pl.when(is_one)(run)
                else:
                    run()

    def rows_of(i):
        return pl.ds(pl.multiple_of(i * ROWS, ROWS), ROWS)

    def hcopy(j, i, side):
        slot = j * chunks + i
        return remote(
            own.at[j, rows_of(i), :], near.at[1 - side, j, rows_of(i), :],
            hsend.at[side, slot], hrecv.at[side, slot], dp, t - 1 if side == 0 else t + 1,
        )

    def exchanged(side, i):
        there, far = ((has_before, far_before), (has_after, far_after))[side]
        return jnp.logical_and(there, jnp.logical_not(jnp.logical_and(far, i < FAR_CHUNKS)))

    def send_hidden(pair, i):
        for side in range(2):
            @pl.when(exchanged(side, i))
            def _():
                for j in pair:
                    hcopy(j, i, side).start()

    far_rows = (FAR_CHUNKS * ROWS // breadth + 1) * breadth
    far_copy = remote(vid_hbm.at[pl.ds(0, far_rows)], vid_far, vsem.at[0], vsem.at[1], dp, far_tile)

    def prepare(src, dst, lines):
        lanes = lax.broadcasted_iota(jnp.int32, (breadth, BLOCK), 1)
        at = lax.broadcasted_iota(jnp.int32, (breadth, group), 0)

        @pl.loop(0, lines)
        def _(r):
            line = src[pl.ds(pl.multiple_of(r * breadth, breadth), breadth), :].astype(jnp.float32)
            rows = pl.ds(pl.multiple_of((r + 1) * breadth, breadth), breadth)
            parts = [line[:, n * BLOCK : (n + 1) * BLOCK] for n in range(blocks)]
            turned = [pltpu.roll(part, shard, 1) for part in parts]
            low = lanes < shard
            for z_at in range(2):
                left_of, right_of = (parts, turned) if z_at == 0 else (turned, parts)
                mid = jnp.concatenate(
                    [jnp.where(low, left_of[n], right_of[n + 1]) for n in range(0, blocks, 2)], axis=1
                )
                left = jnp.where(at == 0, 0.0, pltpu.roll(mid, 1, 0))
                right = jnp.where(at == breadth - 1, 0.0, pltpu.roll(mid, breadth - 1, 0))
                for dx, value in enumerate((left, mid, right)):
                    start = (3 * z_at + dx) * group
                    dst[rows, start : start + group] = value.astype(jnp.bfloat16)

    def half_dot(xs, z_at, pair, i):
        total = None
        for dy in range(3):
            start = pl.multiple_of(i * ROWS + dy * breadth, breadth)
            lhs = xs[pl.ds(start, ROWS), pl.ds(pl.multiple_of(z_at * (3 * group), 3 * group), 3 * group)]
            rhs = jnp.concatenate(
                [wb[j, z_at, 3 * dy : 3 * dy + 3].reshape(3 * group, BLOCK) for j in pair], axis=1
            )
            part = jnp.dot(lhs, rhs, preferred_element_type=jnp.float32)
            total = part if total is None else total + part
        return total

    def activate(total, pair):
        total = total + jnp.concatenate([sb_ref[j] for j in pair], axis=1)
        return (total / (1.0 + jnp.exp(-total))).astype(jnp.bfloat16)

    pairs = (block_a, block_b), (block_c, block_d)

    def spatial_first(p, i):
        acc[rows_of(i), 2 * BLOCK * p : 2 * BLOCK * (p + 1)] = half_dot(xcat, zh, pairs[p], i)

    def spatial_rest(p, i):
        total = acc[rows_of(i), 2 * BLOCK * p : 2 * BLOCK * (p + 1)] + half_dot(xcat, 1 - zh, pairs[p], i)
        hidden = activate(total, pairs[p])
        for n, j in enumerate(pairs[p]):
            own[j, rows_of(i), :] = hidden[:, n * BLOCK : (n + 1) * BLOCK]

    @pl.when(jnp.logical_and(is_one, edge))
    def _():
        for g in range(3):
            start_z(g)

    @pl.when(is_zero)
    def _():
        start_y(0, source(0))
        start_y(1, source(1))

    @pl.when(far_any)
    def _():
        far_copy.start()

    zeros = jnp.zeros((breadth, 6 * group), jnp.bfloat16)
    xcat[0:breadth, :] = zeros
    xcat[breadth + pixels :, :] = zeros
    vid_copy.wait()
    prepare(outv, xcat, height)
    for load in loads:
        load.wait()

    @pl.when(is_zero)
    def _():
        stage_y(0)
        stage_y(1)
        stage_far(0)
        stage_far(1)
        start_y(2, source(2))

    @pl.when(is_one)
    def _():
        stage_z(0)
        stage_z(1)
        stage_done(0, (1, 2, 3))
        stage_done(1, (1, 2, 3))

    def on(flag, n, at, *stages):
        @pl.when(jnp.logical_and(flag, n == at))
        def _():
            for stage in stages:
                stage()

    @pl.loop(0, chunks)
    def _(n):
        spatial_first(0, chunks - 1 - n)
        on(is_zero, n, 0, lambda: stage_x(3), lambda: stage_x(1))
        on(is_zero, n, 1, lambda: stage_x(2))
        on(is_one, n, 0, lambda: stage_y(0))
        on(is_one, n, 1, lambda: stage_y(1))
        on(is_one, n, 2, lambda: stage_far(0))
        on(is_one, n, 3, lambda: stage_far(1))

    @pl.when(is_one)
    def _():
        stage_x_done((1, 2, 3))

    @pl.loop(0, chunks)
    def _(n):
        spatial_first(1, chunks - 1 - n)
        on(is_zero, n, 1, lambda: stage_y(2))
        on(is_zero, n, 3, lambda: stage_far(2))
        on(is_one, n, 0, lambda: stage_x(0), lambda: stage_x(3))
        on(is_one, n, 1, lambda: stage_x(1))
        on(is_one, n, 2, lambda: stage_x(2))
        on(is_one, n, 3, lambda: stage_z(2))

    @pl.when(is_zero)
    def _():
        stage_done(0, range(4))
        stage_done(1, range(4))

    @pl.loop(0, chunks)
    def _(n):
        spatial_rest(0, chunks - 1 - n)

        @pl.when(n > 0)
        def _():
            send_hidden(pairs[0], chunks - n)

        on(is_one, n, 1, lambda: stage_y(2))
        on(is_one, n, 3, lambda: stage_far(2))

    @pl.when(is_zero)
    def _():
        stage_x_done(range(4))

    @pl.loop(0, chunks)
    def _(n):
        spatial_rest(1, chunks - 1 - n)

        @pl.when(n == 0)
        def _():
            send_hidden(pairs[0], 0)

        @pl.when(n > 0)
        def _():
            send_hidden(pairs[1], chunks - n)

    pl.when(is_zero)(lambda: stage_done(2, range(4)))
    pl.when(is_one)(lambda: stage_done(2, (1, 2, 3)))

    def taps(lag, j):
        return wt[lag, columns(j), :]

    def temporal(lag, ref, pair, i):
        lhs = jnp.concatenate([ref[j, rows_of(i), :] for j in pair], axis=1)
        rhs = jnp.concatenate([taps(lag, j) for j in pair], axis=0)
        return jnp.dot(lhs, rhs, preferred_element_type=jnp.float32)

    @pl.loop(0, chunks)
    def _(n):
        acc[rows_of(n), :] = temporal(1, own, pairs[0], n) + temporal(1, own, pairs[1], n) + tb_ref[...]

        @pl.when(n == 0)
        def _():
            send_hidden(pairs[1], 0)

    @pl.when(far_any)
    def _():
        far_copy.wait()
        xcat_far[0:breadth, :] = zeros
        prepare(vid_far, xcat_far, far_rows // breadth)

        @pl.loop(0, 2 * FAR_CHUNKS)
        def _(n):
            p, i = n // FAR_CHUNKS, n % FAR_CHUNKS
            pair = ((x + p) % 4, (x + p + 2) % 4)
            hidden = activate(half_dot(xcat_far, 0, pair, i) + half_dot(xcat_far, 1, pair, i), pair)
            for m, j in enumerate(pair):
                near[far_side, j, rows_of(i), :] = hidden[:, m * BLOCK : (m + 1) * BLOCK]

    x_before, x_after = (t + tiles - 1) % tiles // 8, (t + 1) % tiles // 8
    for p in range(2):
        @pl.loop(0, chunks)
        def _(n, p=p):
            i = chunks - 1 - n
            rows = rows_of(i)
            for side, there, x_there in ((0, has_before, x_before), (1, has_after, x_after)):
                pair = ((x_there + p) % 4, (x_there + p + 2) % 4)

                @pl.when(exchanged(side, i))
                def _():
                    for j in pair:
                        hcopy(j, i, 1 - side).wait_recv()

                @pl.when(there)
                def _():
                    acc[rows, :] += temporal(2 * side, near.at[side], pair, i)

            if p == 1:
                outv[rows, :] = acc[rows, :].astype(jnp.bfloat16)
                pltpu.make_async_copy(outv.at[rows], out_hbm.at[rows], osem.at[i]).start()

    wait_sends()

    @pl.loop(0, chunks)
    def _(i):
        for side in range(2):
            @pl.when(exchanged(side, i))
            def _():
                for j in range(blocks):
                    hcopy(j, i, side).wait_send()

        pltpu.make_async_copy(outv.at[rows_of(i)], out_hbm.at[rows_of(i)], osem.at[i]).wait()


def per_device(videos, spatial_filter, temporal_filter, spatial_bias, temporal_bias):
    _, _, height, breadth, chans = videos.shape
    shard = spatial_filter.shape[1]
    pixels = height * breadth
    blocks = chans // BLOCK
    chunks = pixels // ROWS
    far_pixels = FAR_CHUNKS * ROWS + breadth
    bf = jnp.bfloat16
    anywhere = pl.BlockSpec(memory_space=pl.ANY)
    vmem = pl.BlockSpec(memory_space=pltpu.VMEM)
    dma = pltpu.SemaphoreType.DMA
    out = pl.pallas_call(
        functools.partial(kernel, (height, breadth, chans, shard)),
        out_shape=jax.ShapeDtypeStruct((pixels, chans), bf),
        in_specs=[anywhere, anywhere, anywhere, vmem, vmem],
        out_specs=anywhere,
        scratch_shapes=[
            pltpu.VMEM((pixels + 2 * breadth, 3 * chans), bf),
            pltpu.VMEM((far_pixels + breadth, 3 * chans), bf),
            pltpu.VMEM((far_pixels, chans), bf),
            pltpu.VMEM((blocks, 2, TAPS_S, chans // 2, BLOCK), bf),
            pltpu.VMEM((TAPS_T, chans, chans), bf),
            pltpu.VMEM((blocks, pixels, BLOCK), bf),
            pltpu.VMEM((2, blocks, pixels, BLOCK), bf),
            pltpu.VMEM((pixels, chans), jnp.float32),
            pltpu.VMEM((pixels, chans), bf),
            dma((6,)),
            dma((3, 10)), dma((3, 9)),
            dma((2, 4)), dma((2, 4)),
            dma((2, 4)), dma((2, 4)),
            dma((2, blocks * chunks)), dma((2, blocks * chunks)),
            dma((2,)),
            dma((chunks,)),
        ],
        compiler_params=pltpu.CompilerParams(
            collective_id=0, has_side_effects=True, vmem_limit_bytes=56 * 1024 * 1024
        ),
    )(
        videos.reshape(pixels, chans),
        spatial_filter,
        temporal_filter,
        spatial_bias.reshape(blocks, 1, BLOCK),
        temporal_bias.reshape(1, chans),
    )
    return out.reshape(videos.shape)


def solution(mesh):
    return jax.shard_map(
        per_device,
        mesh=mesh,
        in_specs=(
            P("dp", "tile", None, None, None),
            P(None, "dp", None),
            P(None, "dp", None),
            P(),
            P(),
        ),
        out_specs=P("dp", "tile", None, None, None),
        check_vma=False,
    )
```

time: 84.6 us -> 82.5 us (0.975)
  the two profiles are of different devices: /device:TPU:6 before, /device:TPU:34 now
where the time goes in v3:
time: 82.5 us; the launch traced here: 81.5 us
  Pallas kernels  78.4 us (95%)
  local copies, waits for them, and re-layouts  3.13 us (4%)
    pallas_call x1, Pallas kernels, per_device(): pl.pallas_call(functools.partial(kernel, (height, breadth, chans, shard))...  78.4 us
    unnamed x1, local copies, waits for them, and re-layouts  3.13 us

profile of v3, /device:TPU:34, one launch (start us, length us, event | category | flops | bytes accessed | tf_op | source)
XLA Modules:
  0.0 81.5 jit_solution(4857518411117137665)
XLA Ops:
  0.0 78.4 %shard_map.55 = bf16[2048,512]{1,0:T(8,128)(2,1)} custom-call(bf16[2048,512]{1,0:T(8,128)(2,1)} %bitcast.5, bf16[9,64,512]{2,1,0:T(8,128)(2,1)} %ws_hbm.1, bf16[3,64,512]{2,1,0:T(8,128)(2,1)} %wt_hbm.1, f32[4,1,128]{2,1,0:T(1,128)} %bitcast.6, f32[1,512]{1,0:T(1,128)} %bitcast.7), custom_call_target="tpu_custom_call" | custom-call | tf_op jit(solution)/shard_map/pallas_call | solution.py:455
  78.4 3.1 %copy.7 = bf16[1,1,32,64,512]{4,3,2,1,0:T(8,128)(2,1)} copy(bf16[1,1,32,64,512]{4,3,2,1,0:T(8,128)(2,1)} %bitcast.4) | data formatting | bytes 4194304

commit v4 on v3

--- a/solution.py
+++ b/solution.py
@@ -10,6 +10,7 @@
 BLOCK = 128
 ROWS = 512
 FAR_CHUNKS = 3
+FAR_PARTS = 1
 TAPS_S, TAPS_T = 9, 3
 MESH = pl.DeviceIdType.MESH
 
@@ -50,6 +51,8 @@
     is_zero = core == 0
 
     block_a, block_b, block_c, block_d = x, (x + 2) % 4, (x + 1) % 4, (x + 3) % 4
+    block_e, cross_e = jnp.where(first, block_d, block_c), jnp.where(first, block_c, block_d)
+    ring_blocks = {0: block_a, 1: block_b, 3: block_e}
     carried = jnp.where(is_zero, zh, 1 - zh)
 
     def remote(src, dst, ssem, rsem, to_dp, to_tile):
@@ -66,13 +69,13 @@
         return wb.at[j, z_at, :, pl.ds(pl.multiple_of(y_at * shard + low, half), count), :]
 
     def piece(g, y_at, z_at, low=0, count=None):
-        if g < 2:
-            return block_piece((block_a, block_b)[g], y_at, z_at, low, count)
+        if g != 2:
+            return block_piece(ring_blocks[g], y_at, z_at, low, count)
         count = shard if count is None else count
         return wt.at[:, pl.ds(pl.multiple_of((y_at * 2 + z_at) * shard + low, half), count), :]
 
     def source(g):
-        return wt_hbm if g == 2 else ws_hbm.at[:, :, columns((block_a, block_b)[g])]
+        return wt_hbm if g == 2 else ws_hbm.at[:, :, columns(ring_blocks[g])]
 
     vid_copy = pltpu.make_async_copy(vid_hbm, outv, local_sem.at[5])
     loads = [
@@ -123,16 +126,27 @@
         ref = block_piece(block_a, y_at, carried)
         return remote(ref, ref, xsend.at[n, k], xrecv.at[n, k], dp, to_tile)
 
+    by_x = jnp.logical_not(first), jnp.logical_not(last)
+
     def y_of(k):
         return (y + k) % 4
 
     def spread(g, k):
         ring(g, 6 + k, 5 + k, y_of(k), carried, dp, partner).start()
         if g == 0:
-            from_x(0, k, y_of(k), x_next).start()
-            from_x(1, k, y_of(k), x_prev).start()
+            pl.when(by_x[0])(lambda: from_x(0, k, y_of(k), x_next).start())
+            pl.when(by_x[1])(lambda: from_x(1, k, y_of(k), x_prev).start())
+
+    def cross_copy():
+        return remote(
+            ws_hbm.at[:, :, columns(cross_e)], block_piece(cross_e, y, zh), wsend.at[3, 0], wrecv.at[3, 0],
+            other, cross_edge,
+        )
 
     def start_z(g):
+        if g == 3:
+            cross_copy().start()
+            return
         ring(g, 1, 0, y, zh, other, cross_inner, src=source(g)).start()
         ring(g, 0, 0, y, zh, other, cross_edge, src=source(g)).start()
 
@@ -168,38 +182,56 @@
 
     def stage_x(k):
         for n in range(2):
-            ref = block_piece((block_d, block_c)[n], y_of(k), carried)
-            remote(ref, ref, xsend.at[n, k], xrecv.at[n, k], dp, x_next).wait_recv()
-            onward(n, k, carried).start()
+            @pl.when(by_x[n])
+            def _():
+                ref = block_piece((block_d, block_c)[n], y_of(k), carried)
+                remote(ref, ref, xsend.at[n, k], xrecv.at[n, k], dp, x_next).wait_recv()
+                onward(n, k, carried).start()
 
     def stage_x_done(ks):
-        for k in ks:
-            for n in range(2):
-                onward(n, k, 1 - carried).wait_recv()
+        for n in range(2):
+            @pl.when(by_x[n])
+            def _():
+                for k in ks:
+                    onward(n, k, 1 - carried).wait_recv()
+
+        pl.when(edge)(lambda: stage_done(3, ks))
+
+    def wait_ring(g):
+        for slot in (2, 3):
+            ring(g, slot, 0, y, carried, up, t).wait_send()
+        for slot in (4, 5):
+            ring(g, slot, 0, y, carried, up, t, 0, half).wait_send()
+        for k in range(1, 4):
+            ring(g, 6 + k, 5 + k, y, carried, dp, partner).wait_send()
+
+        @pl.when(is_one)
+        def _():
+            ring(g, 6, 5, y, carried, dp, partner).wait_send()
 
     def wait_sends():
         for g in range(3):
-            @pl.when(jnp.logical_and(is_one, edge))
-            def _():
+            wait_ring(g)
+        pl.when(edge)(lambda: wait_ring(3))
+
+        @pl.when(jnp.logical_and(is_one, edge))
+        def _():
+            for g in range(3):
                 ring(g, 0, 0, y, zh, other, cross_edge).wait_send()
                 ring(g, 1, 0, y, zh, other, cross_inner).wait_send()
-
-            for slot in (2, 3):
-                ring(g, slot, 0, y, carried, up, t).wait_send()
-            for slot in (4, 5):
-                ring(g, slot, 0, y, carried, up, t, 0, half).wait_send()
-            for k in range(4):
-                def run():
-                    ring(g, 6 + k, 5 + k, y, carried, dp, partner).wait_send()
-                    if g == 0:
-                        for n in range(2):
-                            from_x(n, k, y, x_next).wait_send()
-                            onward(n, k, carried).wait_send()
-
-                if k == 0:
-                    pl.when(is_one)(run)
-                else:
-                    run()
+            cross_copy().wait_send()
+
+        def wait_x(n, k):
+            from_x(n, k, y, x_next).wait_send()
+            onward(n, k, carried).wait_send()
+
+        for n in range(2):
+            @pl.when(by_x[n])
+            def _():
+                for k in range(1, 4):
+                    wait_x(n, k)
+
+            pl.when(jnp.logical_and(by_x[n], is_one))(lambda: wait_x(n, 0))
 
     def rows_of(i):
         return pl.ds(pl.multiple_of(i * ROWS, ROWS), ROWS)
@@ -223,7 +255,14 @@
                     hcopy(j, i, side).start()
 
     far_rows = (FAR_CHUNKS * ROWS // breadth + 1) * breadth
-    far_copy = remote(vid_hbm.at[pl.ds(0, far_rows)], vid_far, vsem.at[0], vsem.at[1], dp, far_tile)
+    far_cuts = [far_rows * n // (FAR_PARTS * breadth) * breadth for n in range(FAR_PARTS + 1)]
+
+    def far_copy(n):
+        rows = pl.ds(far_cuts[n], far_cuts[n + 1] - far_cuts[n])
+        return remote(vid_hbm.at[rows], vid_far.at[rows], vsem.at[0, n], vsem.at[1, n], dp, far_tile)
+
+    def far_start(n):
+        pl.when(far_any)(lambda: far_copy(n).start())
 
     def prepare(src, dst, lines):
         lanes = lax.broadcasted_iota(jnp.int32, (breadth, BLOCK), 1)
@@ -276,7 +315,7 @@
 
     @pl.when(jnp.logical_and(is_one, edge))
     def _():
-        for g in range(3):
+        for g in (0, 1, 3, 2):
             start_z(g)
 
     @pl.when(is_zero)
@@ -284,9 +323,7 @@
         start_y(0, source(0))
         start_y(1, source(1))
 
-    @pl.when(far_any)
-    def _():
-        far_copy.start()
+    far_start(0)
 
     zeros = jnp.zeros((breadth, 6 * group), jnp.bfloat16)
     xcat[0:breadth, :] = zeros
@@ -302,14 +339,18 @@
         stage_y(1)
         stage_far(0)
         stage_far(1)
-        start_y(2, source(2))
+        pl.when(edge)(lambda: start_y(3, source(3)))
 
     @pl.when(is_one)
     def _():
         stage_z(0)
         stage_z(1)
+        stage_y(0)
+        stage_y(1)
         stage_done(0, (1, 2, 3))
         stage_done(1, (1, 2, 3))
+
+    edge_zero, edge_one = jnp.logical_and(edge, is_zero), jnp.logical_and(edge, is_one)
 
     def on(flag, n, at, *stages):
         @pl.when(jnp.logical_and(flag, n == at))
@@ -320,81 +361,68 @@
     @pl.loop(0, chunks)
     def _(n):
         spatial_first(0, chunks - 1 - n)
-        on(is_zero, n, 0, lambda: stage_x(3), lambda: stage_x(1))
-        on(is_zero, n, 1, lambda: stage_x(2))
-        on(is_one, n, 0, lambda: stage_y(0))
-        on(is_one, n, 1, lambda: stage_y(1))
-        on(is_one, n, 2, lambda: stage_far(0))
-        on(is_one, n, 3, lambda: stage_far(1))
-
-    @pl.when(is_one)
-    def _():
-        stage_x_done((1, 2, 3))
+        on(is_zero, n, 1, lambda: stage_x(3))
+        on(is_zero, n, 2, lambda: stage_x(1))
+        on(is_zero, n, 3, lambda: stage_x(2))
+        on(is_one, n, 0, lambda: stage_far(0))
+        on(is_one, n, 1, lambda: stage_far(1))
+        on(edge_one, n, 2, lambda: stage_z(3))
+
+    @pl.when(is_zero)
+    def _():
+        stage_done(0, range(4))
+        stage_done(1, range(4))
+
+    @pl.loop(0, chunks)
+    def _(n):
+        spatial_rest(0, chunks - 1 - n)
+
+        @pl.when(n > 0)
+        def _():
+            send_hidden(pairs[0], chunks - n)
+
+        on(is_zero, n, 0, lambda: start_y(2, source(2)))
+        on(edge_zero, n, 0, lambda: stage_y(3))
+        on(is_one, n, 0, lambda: stage_x(0))
+        on(is_one, n, 1, lambda: stage_x(3))
+        on(edge_one, n, 1, lambda: stage_y(3))
+        on(is_one, n, 2, lambda: stage_x(1))
+        on(edge_zero, n, 3, lambda: stage_far(3))
+
+    pl.when(is_one)(lambda: stage_x_done((1, 2, 3)))
 
     @pl.loop(0, chunks)
     def _(n):
         spatial_first(1, chunks - 1 - n)
-        on(is_zero, n, 1, lambda: stage_y(2))
-        on(is_zero, n, 3, lambda: stage_far(2))
-        on(is_one, n, 0, lambda: stage_x(0), lambda: stage_x(3))
-        on(is_one, n, 1, lambda: stage_x(1))
-        on(is_one, n, 2, lambda: stage_x(2))
-        on(is_one, n, 3, lambda: stage_z(2))
-
-    @pl.when(is_zero)
-    def _():
-        stage_done(0, range(4))
-        stage_done(1, range(4))
-
-    @pl.loop(0, chunks)
-    def _(n):
-        spatial_rest(0, chunks - 1 - n)
-
-        @pl.when(n > 0)
+
+        @pl.when(n == 0)
         def _():
-            send_hidden(pairs[0], chunks - n)
-
-        on(is_one, n, 1, lambda: stage_y(2))
-        on(is_one, n, 3, lambda: stage_far(2))
-
-    @pl.when(is_zero)
-    def _():
-        stage_x_done(range(4))
+            send_hidden(pairs[0], 0)
+
+        on(is_one, n, 0, lambda: stage_x(2))
+        on(edge_one, n, 1, lambda: stage_far(3))
+        on(is_one, n, 2, lambda: stage_z(2))
+
+    pl.when(is_zero)(lambda: stage_x_done(range(4)))
 
     @pl.loop(0, chunks)
     def _(n):
         spatial_rest(1, chunks - 1 - n)
 
-        @pl.when(n == 0)
-        def _():
-            send_hidden(pairs[0], 0)
-
         @pl.when(n > 0)
         def _():
             send_hidden(pairs[1], chunks - n)
 
-    pl.when(is_zero)(lambda: stage_done(2, range(4)))
-    pl.when(is_one)(lambda: stage_done(2, (1, 2, 3)))
-
-    def taps(lag, j):
-        return wt[lag, columns(j), :]
-
-    def temporal(lag, ref, pair, i):
-        lhs = jnp.concatenate([ref[j, rows_of(i), :] for j in pair], axis=1)
-        rhs = jnp.concatenate([taps(lag, j) for j in pair], axis=0)
-        return jnp.dot(lhs, rhs, preferred_element_type=jnp.float32)
-
-    @pl.loop(0, chunks)
-    def _(n):
-        acc[rows_of(n), :] = temporal(1, own, pairs[0], n) + temporal(1, own, pairs[1], n) + tb_ref[...]
-
-        @pl.when(n == 0)
-        def _():
-            send_hidden(pairs[1], 0)
+        on(is_zero, n, 1, lambda: stage_y(2))
+        on(is_one, n, 2, lambda: stage_y(2))
+
+    stage_far(2)
+    send_hidden(pairs[1], 0)
 
     @pl.when(far_any)
     def _():
-        far_copy.wait()
+        for n in range(FAR_PARTS):
+            far_copy(n).wait()
         xcat_far[0:breadth, :] = zeros
         prepare(vid_far, xcat_far, far_rows // breadth)
 
@@ -405,6 +433,21 @@
             hidden = activate(half_dot(xcat_far, 0, pair, i) + half_dot(xcat_far, 1, pair, i), pair)
             for m, j in enumerate(pair):
                 near[far_side, j, rows_of(i), :] = hidden[:, m * BLOCK : (m + 1) * BLOCK]
+
+    pl.when(is_zero)(lambda: stage_done(2, range(4)))
+    pl.when(is_one)(lambda: stage_done(2, (1, 2, 3)))
+
+    def taps(lag, j):
+        return wt[lag, columns(j), :]
+
+    def temporal(lag, ref, pair, i):
+        lhs = jnp.concatenate([ref[j, rows_of(i), :] for j in pair], axis=1)
+        rhs = jnp.concatenate([taps(lag, j) for j in pair], axis=0)
+        return jnp.dot(lhs, rhs, preferred_element_type=jnp.float32)
+
+    @pl.loop(0, chunks)
+    def _(n):
+        acc[rows_of(n), :] = temporal(1, own, pairs[0], n) + temporal(1, own, pairs[1], n) + tb_ref[...]
 
     x_before, x_after = (t + tiles - 1) % tiles // 8, (t + 1) % tiles // 8
     for p in range(2):
@@ -468,11 +511,11 @@
             pltpu.VMEM((pixels, chans), jnp.float32),
             pltpu.VMEM((pixels, chans), bf),
             dma((6,)),
-            dma((3, 10)), dma((3, 9)),
+            dma((4, 10)), dma((4, 9)),
             dma((2, 4)), dma((2, 4)),
             dma((2, 4)), dma((2, 4)),
             dma((2, blocks * chunks)), dma((2, blocks * chunks)),
-            dma((2,)),
+            dma((2, FAR_PARTS)),
             dma((chunks,)),
         ],
         compiler_params=pltpu.CompilerParams(

time: 82.5 us -> 68.8 us (0.83)
  the two profiles are of different devices: /device:TPU:34 before, /device:TPU:2 now
where the time goes in v4:
time: 68.8 us; the launch traced here: 68.7 us
  Pallas kernels  65.5 us (95%)
  local copies, waits for them, and re-layouts  3.13 us (5%)
    pallas_call x1, Pallas kernels, per_device(): pl.pallas_call(functools.partial(kernel, (height, breadth, chans, shard))...  65.5 us
    unnamed x1, local copies, waits for them, and re-layouts  3.13 us

profile of v4, /device:TPU:2, one launch (start us, length us, event | category | flops | bytes accessed | tf_op | source)
XLA Modules:
  0.0 68.7 jit_solution(17032355016899004307)
XLA Ops:
  0.0 65.5 %shard_map.55 = bf16[2048,512]{1,0:T(8,128)(2,1)} custom-call(bf16[2048,512]{1,0:T(8,128)(2,1)} %bitcast.5, bf16[9,64,512]{2,1,0:T(8,128)(2,1)} %ws_hbm.1, bf16[3,64,512]{2,1,0:T(8,128)(2,1)} %wt_hbm.1, f32[4,1,128]{2,1,0:T(1,128)} %bitcast.6, f32[1,512]{1,0:T(1,128)} %bitcast.7), custom_call_target="tpu_custom_call" | custom-call | tf_op jit(solution)/shard_map/pallas_call | solution.py:498
  65.6 3.1 %copy.7 = bf16[1,1,32,64,512]{4,3,2,1,0:T(8,128)(2,1)} copy(bf16[1,1,32,64,512]{4,3,2,1,0:T(8,128)(2,1)} %bitcast.4) | data formatting | bytes 4194304

commit v5 on v4

--- a/solution.py
+++ b/solution.py
@@ -9,16 +9,16 @@
 
 BLOCK = 128
 ROWS = 512
-FAR_CHUNKS = 3
+FAR_CHUNKS = 2
 FAR_PARTS = 1
 TAPS_S, TAPS_T = 9, 3
 MESH = pl.DeviceIdType.MESH
 
 
 def kernel(
-    dims, vid_hbm, ws_hbm, wt_hbm, sb_ref, tb_ref, out_hbm,
-    xcat, xcat_far, vid_far, wb, wt, own, near, acc, outv,
-    local_sem, wsend, wrecv, xsend, xrecv, psend, precv, hsend, hrecv, vsem, osem,
+    dims, vid_hbm, ws_hbm, wt_hbm, sb_hbm, tb_hbm, outv,
+    xcat, xcat_far, vid_far, wb, wt, own, near, acc, sb_ref, tb_ref,
+    local_sem, wsend, wrecv, xsend, xrecv, psend, precv, hsend, hrecv, vsem,
 ):
     height, breadth, chans, shard = dims
     pixels = height * breadth
@@ -83,6 +83,8 @@
         for n, j in enumerate((block_a, block_b, block_c, block_d))
     ]
     loads.append(pltpu.make_async_copy(wt_hbm, piece(2, y, zh), local_sem.at[4]))
+    loads.append(pltpu.make_async_copy(sb_hbm, sb_ref, local_sem.at[6]))
+    loads.append(pltpu.make_async_copy(tb_hbm, tb_ref, local_sem.at[7]))
     vid_copy.start()
     for load in loads:
         load.start()
@@ -236,10 +238,10 @@
     def rows_of(i):
         return pl.ds(pl.multiple_of(i * ROWS, ROWS), ROWS)
 
-    def hcopy(j, i, side):
-        slot = j * chunks + i
+    def hcopy(q, i, side):
+        slot = q * chunks + i
         return remote(
-            own.at[j, rows_of(i), :], near.at[1 - side, j, rows_of(i), :],
+            own.at[q, :, rows_of(i), :], near.at[1 - side, q, :, rows_of(i), :],
             hsend.at[side, slot], hrecv.at[side, slot], dp, t - 1 if side == 0 else t + 1,
         )
 
@@ -247,12 +249,9 @@
         there, far = ((has_before, far_before), (has_after, far_after))[side]
         return jnp.logical_and(there, jnp.logical_not(jnp.logical_and(far, i < FAR_CHUNKS)))
 
-    def send_hidden(pair, i):
+    def send_hidden(p, i):
         for side in range(2):
-            @pl.when(exchanged(side, i))
-            def _():
-                for j in pair:
-                    hcopy(j, i, side).start()
+            pl.when(exchanged(side, i))(lambda: hcopy((x + p) % 2, i, side).start())
 
     far_rows = (FAR_CHUNKS * ROWS // breadth + 1) * breadth
     far_cuts = [far_rows * n // (FAR_PARTS * breadth) * breadth for n in range(FAR_PARTS + 1)]
@@ -311,7 +310,7 @@
         total = acc[rows_of(i), 2 * BLOCK * p : 2 * BLOCK * (p + 1)] + half_dot(xcat, 1 - zh, pairs[p], i)
         hidden = activate(total, pairs[p])
         for n, j in enumerate(pairs[p]):
-            own[j, rows_of(i), :] = hidden[:, n * BLOCK : (n + 1) * BLOCK]
+            own[j % 2, j // 2, rows_of(i), :] = hidden[:, n * BLOCK : (n + 1) * BLOCK]
 
     @pl.when(jnp.logical_and(is_one, edge))
     def _():
@@ -379,7 +378,7 @@
 
         @pl.when(n > 0)
         def _():
-            send_hidden(pairs[0], chunks - n)
+            send_hidden(0, chunks - n)
 
         on(is_zero, n, 0, lambda: start_y(2, source(2)))
         on(edge_zero, n, 0, lambda: stage_y(3))
@@ -397,7 +396,7 @@
 
         @pl.when(n == 0)
         def _():
-            send_hidden(pairs[0], 0)
+            send_hidden(0, 0)
 
         on(is_one, n, 0, lambda: stage_x(2))
         on(edge_one, n, 1, lambda: stage_far(3))
@@ -411,13 +410,13 @@
 
         @pl.when(n > 0)
         def _():
-            send_hidden(pairs[1], chunks - n)
+            send_hidden(1, chunks - n)
 
         on(is_zero, n, 1, lambda: stage_y(2))
         on(is_one, n, 2, lambda: stage_y(2))
 
     stage_far(2)
-    send_hidden(pairs[1], 0)
+    send_hidden(1, 0)
 
     @pl.when(far_any)
     def _():
@@ -432,7 +431,7 @@
             pair = ((x + p) % 4, (x + p + 2) % 4)
             hidden = activate(half_dot(xcat_far, 0, pair, i) + half_dot(xcat_far, 1, pair, i), pair)
             for m, j in enumerate(pair):
-                near[far_side, j, rows_of(i), :] = hidden[:, m * BLOCK : (m + 1) * BLOCK]
+                near[far_side, j % 2, j // 2, rows_of(i), :] = hidden[:, m * BLOCK : (m + 1) * BLOCK]
 
     pl.when(is_zero)(lambda: stage_done(2, range(4)))
     pl.when(is_one)(lambda: stage_done(2, (1, 2, 3)))
@@ -440,14 +439,16 @@
     def taps(lag, j):
         return wt[lag, columns(j), :]
 
-    def temporal(lag, ref, pair, i):
-        lhs = jnp.concatenate([ref[j, rows_of(i), :] for j in pair], axis=1)
-        rhs = jnp.concatenate([taps(lag, j) for j in pair], axis=0)
+    def temporal(lag, ref, q, i):
+        lhs = jnp.concatenate([ref[q, m, rows_of(i), :] for m in range(2)], axis=1)
+        rhs = jnp.concatenate([taps(lag, q), taps(lag, q + 2)], axis=0)
         return jnp.dot(lhs, rhs, preferred_element_type=jnp.float32)
 
     @pl.loop(0, chunks)
     def _(n):
-        acc[rows_of(n), :] = temporal(1, own, pairs[0], n) + temporal(1, own, pairs[1], n) + tb_ref[...]
+        acc[rows_of(n), :] = temporal(1, own, 0, n) + temporal(1, own, 1, n) + tb_ref[...]
+
+    wait_sends()
 
     x_before, x_after = (t + tiles - 1) % tiles // 8, (t + 1) % tiles // 8
     for p in range(2):
@@ -456,32 +457,23 @@
             i = chunks - 1 - n
             rows = rows_of(i)
             for side, there, x_there in ((0, has_before, x_before), (1, has_after, x_after)):
-                pair = ((x_there + p) % 4, (x_there + p + 2) % 4)
-
-                @pl.when(exchanged(side, i))
-                def _():
-                    for j in pair:
-                        hcopy(j, i, 1 - side).wait_recv()
+                q = (x_there + p) % 2
+                pl.when(exchanged(side, i))(lambda: hcopy(q, i, 1 - side).wait_recv())
 
                 @pl.when(there)
                 def _():
-                    acc[rows, :] += temporal(2 * side, near.at[side], pair, i)
+                    acc[rows, :] += temporal(2 * side, near.at[side], q, i)
 
             if p == 1:
                 outv[rows, :] = acc[rows, :].astype(jnp.bfloat16)
-                pltpu.make_async_copy(outv.at[rows], out_hbm.at[rows], osem.at[i]).start()
-
-    wait_sends()
 
     @pl.loop(0, chunks)
     def _(i):
         for side in range(2):
             @pl.when(exchanged(side, i))
             def _():
-                for j in range(blocks):
-                    hcopy(j, i, side).wait_send()
-
-        pltpu.make_async_copy(outv.at[rows_of(i)], out_hbm.at[rows_of(i)], osem.at[i]).wait()
+                for q in range(2):
+                    hcopy(q, i, side).wait_send()
 
 
 def per_device(videos, spatial_filter, temporal_filter, spatial_bias, temporal_bias):
@@ -497,26 +489,26 @@
     dma = pltpu.SemaphoreType.DMA
     out = pl.pallas_call(
         functools.partial(kernel, (height, breadth, chans, shard)),
-        out_shape=jax.ShapeDtypeStruct((pixels, chans), bf),
-        in_specs=[anywhere, anywhere, anywhere, vmem, vmem],
-        out_specs=anywhere,
+        out_shape=pltpu.VMEM((pixels, chans), bf),
+        in_specs=[anywhere] * 5,
+        out_specs=vmem,
         scratch_shapes=[
             pltpu.VMEM((pixels + 2 * breadth, 3 * chans), bf),
             pltpu.VMEM((far_pixels + breadth, 3 * chans), bf),
             pltpu.VMEM((far_pixels, chans), bf),
             pltpu.VMEM((blocks, 2, TAPS_S, chans // 2, BLOCK), bf),
             pltpu.VMEM((TAPS_T, chans, chans), bf),
-            pltpu.VMEM((blocks, pixels, BLOCK), bf),
-            pltpu.VMEM((2, blocks, pixels, BLOCK), bf),
+            pltpu.VMEM((2, blocks // 2, pixels, BLOCK), bf),
+            pltpu.VMEM((2, 2, blocks // 2, pixels, BLOCK), bf),
             pltpu.VMEM((pixels, chans), jnp.float32),
-            pltpu.VMEM((pixels, chans), bf),
-            dma((6,)),
+            pltpu.VMEM((blocks, 1, BLOCK), jnp.float32),
+            pltpu.VMEM((1, chans), jnp.float32),
+            dma((8,)),
             dma((4, 10)), dma((4, 9)),
             dma((2, 4)), dma((2, 4)),
             dma((2, 4)), dma((2, 4)),
-            dma((2, blocks * chunks)), dma((2, blocks * chunks)),
+            dma((2, 2 * chunks)), dma((2, 2 * chunks)),
             dma((2, FAR_PARTS)),
-            dma((chunks,)),
         ],
         compiler_params=pltpu.CompilerParams(
             collective_id=0, has_side_effects=True, vmem_limit_bytes=56 * 1024 * 1024

time: 68.8 us -> 67 us (0.974)
  the two profiles are of different devices: /device:TPU:2 before, /device:TPU:34 now
where the time goes in v5:
time: 67 us; the launch traced here: 66.9 us
  Pallas kernels  65.6 us (98%)
  local copies, waits for them, and re-layouts  1.32 us (2%)
    pallas_call x1, Pallas kernels, per_device(): pl.pallas_call(functools.partial(kernel, (height, breadth, chans, shard))...  65.6 us

profile of v5, /device:TPU:34, one launch (start us, length us, event | category | flops | bytes accessed | tf_op | source)
XLA Modules:
  0.0 66.9 jit_solution(8449320389969287399)
XLA Ops:
  0.0 65.6 %shard_map.55 = bf16[2048,512]{1,0:T(8,128)(2,1)S(1)} custom-call(bf16[2048,512]{1,0:T(8,128)(2,1)} %bitcast.5, bf16[9,64,512]{2,1,0:T(8,128)(2,1)} %ws_hbm.1, bf16[3,64,512]{2,1,0:T(8,128)(2,1)} %wt_hbm.1, f32[4,1,128]{2,1,0:T(1,128)} %bitcast.6, f32[1,512]{1,0:T(1,128)} %bitcast.7), custom_call_target="tpu_custom_call" | custom-call | tf_op jit(solution)/shard_map/pallas_call | solution.py:490
  65.6 1.3 %copy.7 = bf16[1,1,32,64,512]{4,3,2,1,0:T(8,128)(2,1)} copy(bf16[1,1,32,64,512]{4,3,2,1,0:T(8,128)(2,1)S(1)} %bitcast.4) | data formatting | bytes 4194304

commit v6 on v5

--- a/solution.py
+++ b/solution.py
@@ -10,15 +10,16 @@
 BLOCK = 128
 ROWS = 512
 FAR_CHUNKS = 2
-FAR_PARTS = 1
+RELAYED = 3
+FLOWS = 3
 TAPS_S, TAPS_T = 9, 3
 MESH = pl.DeviceIdType.MESH
 
 
 def kernel(
     dims, vid_hbm, ws_hbm, wt_hbm, sb_hbm, tb_hbm, outv,
-    xcat, xcat_far, vid_far, wb, wt, own, near, acc, sb_ref, tb_ref,
-    local_sem, wsend, wrecv, xsend, xrecv, psend, precv, hsend, hrecv, vsem,
+    xcat, xcat_far, vid_far, relayed, made, wb, wt, own, near, acc, sb_ref, tb_ref,
+    local_sem, wsend, wrecv, xsend, xrecv, psend, precv, hsend, hrecv, vsem, rsem, csend, crecv,
 ):
     height, breadth, chans, shard = dims
     pixels = height * breadth
@@ -45,8 +46,20 @@
     far_before = jnp.logical_and(t % 8 == 0, has_before)
     far_after = jnp.logical_and(t % 8 == 7, has_after)
     far_any = jnp.logical_or(far_before, far_after)
-    far_side = jnp.where(far_after, 1, 0)
+    aid_before = jnp.logical_and(t % 8 == 1, t > 1)
+    aid_after = jnp.logical_and(t % 8 == 6, t < tiles - 2)
+    aid_any = jnp.logical_or(aid_before, aid_after)
+    team = jnp.logical_or(far_any, aid_any)
+    far_side = jnp.where(jnp.logical_or(far_after, aid_after), 1, 0)
+    two_off = jnp.where(far_side == 1, t + 2, t - 2)
+    feeding_relay = jnp.where(aid_after, 0, tiles - 1)
     far_tile = jnp.where(far_after, t + 1, t - 1)
+    is_relay = jnp.logical_or(t == 0, t == tiles - 1)
+    my_relay = jnp.where(far_after, tiles - 1, 0)
+    flow = jnp.where(far_after, x, x - 1)
+    x_free = jnp.where(jnp.logical_or(first, zl == 2), FLOWS, 0)
+    in_free = x == x_free
+    x_across = (t + 16) % tiles
     is_one = core == 1
     is_zero = core == 0
 
@@ -99,6 +112,25 @@
     greet(dn, t)
     greet(dp, x_next)
     greet(dp, x_prev)
+    greet(dp, x_across)
+
+    @pl.when(far_any)
+    def _():
+        greet(dp, my_relay)
+
+    @pl.when(aid_any)
+    def _():
+        greet(dp, feeding_relay)
+
+    @pl.when(team)
+    def _():
+        greet(dp, two_off)
+
+    @pl.when(is_relay)
+    def _():
+        for n in range(FLOWS):
+            greet(dp, jnp.where(t == 0, 8 * n + 8, 8 * n + 7))
+            greet(dp, jnp.where(t == 0, 8 * n + 6, 8 * n + 9))
 
     @pl.when(edge)
     def _():
@@ -118,7 +150,7 @@
         greet(dp, t + 1)
 
     one = lambda flag: jnp.where(flag, 1, 0)
-    pl.semaphore_wait(barrier, 6 + one(edge) + one(has_before) + one(has_after))
+    pl.semaphore_wait(barrier, 7 + one(edge) + one(has_before) + one(has_after) + 2 * one(team) + 2 * FLOWS * one(is_relay))
 
     def ring(g, send, recv, y_at, z_at, to_dp, to_tile, low=0, count=None, src=None):
         ref = piece(g, y_at, z_at, low, count)
@@ -149,15 +181,33 @@
         if g == 3:
             cross_copy().start()
             return
-        ring(g, 1, 0, y, zh, other, cross_inner, src=source(g)).start()
+        inner = lambda: ring(g, 1, 0, y, zh, other, cross_inner, src=source(g)).start()
+        if g == 2:
+            pl.when(in_free)(inner)
+        else:
+            inner()
         ring(g, 0, 0, y, zh, other, cross_edge, src=source(g)).start()
 
     def start_y(g, src=None):
         ring(g, 2, 1, y, carried, up, t, src=src).start()
         ring(g, 3, 2, y, carried, dn, t, src=src).start()
 
+    inner_source_of_two = jnp.logical_and(jnp.logical_not(edge), in_free)
+
+    def share(slot, to_tile):
+        return ring(2, slot, 0, y, 1 - zh, dp, to_tile)
+
+    def stage_share():
+        ring(2, 0, 0, y, 1 - zh, dp, partner).wait_recv()
+        for slot, to_tile in ((0, x_next), (1, x_prev), (10, x_across)):
+            share(slot, to_tile).start()
+
     def stage_z(g):
-        ring(g, 0, 0, y, 1 - zh, dp, partner).wait_recv()
+        arrived = lambda: ring(g, 0, 0, y, 1 - zh, dp, partner).wait_recv()
+        if g == 2:
+            pl.when(jnp.logical_not(inner_source_of_two))(arrived)
+        else:
+            arrived()
         start_y(g)
         spread(g, 0)
 
@@ -220,8 +270,15 @@
         def _():
             for g in range(3):
                 ring(g, 0, 0, y, zh, other, cross_edge).wait_send()
+            for g in range(2):
                 ring(g, 1, 0, y, zh, other, cross_inner).wait_send()
+            pl.when(in_free)(lambda: ring(2, 1, 0, y, zh, other, cross_inner).wait_send())
             cross_copy().wait_send()
+
+        @pl.when(jnp.logical_and(is_one, inner_source_of_two))
+        def _():
+            for slot in (0, 1, 10):
+                share(slot, x_next).wait_send()
 
         def wait_x(n, k):
             from_x(n, k, y, x_next).wait_send()
@@ -245,32 +302,52 @@
             hsend.at[side, slot], hrecv.at[side, slot], dp, t - 1 if side == 0 else t + 1,
         )
 
-    def exchanged(side, i):
+    def exchanged(side):
         there, far = ((has_before, far_before), (has_after, far_after))[side]
-        return jnp.logical_and(there, jnp.logical_not(jnp.logical_and(far, i < FAR_CHUNKS)))
+        return jnp.logical_and(there, jnp.logical_not(far))
 
     def send_hidden(p, i):
         for side in range(2):
-            pl.when(exchanged(side, i))(lambda: hcopy((x + p) % 2, i, side).start())
+            pl.when(exchanged(side))(lambda: hcopy((x + p) % 2, i, side).start())
 
     far_rows = (FAR_CHUNKS * ROWS // breadth + 1) * breadth
-    far_cuts = [far_rows * n // (FAR_PARTS * breadth) * breadth for n in range(FAR_PARTS + 1)]
-
-    def far_copy(n):
-        rows = pl.ds(far_cuts[n], far_cuts[n + 1] - far_cuts[n])
-        return remote(vid_hbm.at[rows], vid_far.at[rows], vsem.at[0, n], vsem.at[1, n], dp, far_tile)
-
-    def far_start(n):
-        pl.when(far_any)(lambda: far_copy(n).start())
-
-    def prepare(src, dst, lines):
+    low_from = pixels - far_rows
+    kept = far_rows - RELAYED * breadth
+    passed = pl.ds(low_from + kept, RELAYED * breadth)
+
+    def far_upper():
+        rows = pl.ds(0, far_rows)
+        return remote(vid_hbm.at[rows], vid_far.at[rows], vsem.at[0, 0], vsem.at[1, 0], dp, far_tile)
+
+    def far_lower():
+        return remote(
+            vid_hbm.at[pl.ds(low_from, kept)], vid_far.at[pl.ds(0, kept)], vsem.at[0, 1], vsem.at[1, 1], dp, two_off
+        )
+
+    def to_relay():
+        return remote(vid_hbm.at[passed], relayed.at[flow], vsem.at[0, 2], rsem.at[0, flow], dp, my_relay)
+
+    def from_relay(n, to_tile):
+        return remote(
+            relayed.at[n], vid_far.at[pl.ds(kept, RELAYED * breadth)], rsem.at[1, n], vsem.at[1, 2], dp, to_tile
+        )
+
+    def relay_pass(distance):
+        n = jnp.where(t == 0, distance - 1, FLOWS - distance)
+
+        @pl.when(is_relay)
+        def _():
+            remote(vid_hbm.at[passed], relayed.at[n], vsem.at[0, 2], rsem.at[0, n], dp, partner).wait_recv()
+            from_relay(n, jnp.where(t == 0, 8 * n + 6, 8 * n + 9)).start()
+
+    def prepare(src, dst, lines, above=1):
         lanes = lax.broadcasted_iota(jnp.int32, (breadth, BLOCK), 1)
         at = lax.broadcasted_iota(jnp.int32, (breadth, group), 0)
 
         @pl.loop(0, lines)
         def _(r):
             line = src[pl.ds(pl.multiple_of(r * breadth, breadth), breadth), :].astype(jnp.float32)
-            rows = pl.ds(pl.multiple_of((r + 1) * breadth, breadth), breadth)
+            rows = pl.ds(pl.multiple_of((r + above) * breadth, breadth), breadth)
             parts = [line[:, n * BLOCK : (n + 1) * BLOCK] for n in range(blocks)]
             turned = [pltpu.roll(part, shard, 1) for part in parts]
             low = lanes < shard
@@ -321,8 +398,14 @@
     def _():
         start_y(0, source(0))
         start_y(1, source(1))
-
-    far_start(0)
+        pl.when(edge)(lambda: start_y(3, source(3)))
+
+    @pl.when(far_any)
+    def _():
+        to_relay().start()
+        far_upper().start()
+        far_lower().start()
+
 
     zeros = jnp.zeros((breadth, 6 * group), jnp.bfloat16)
     xcat[0:breadth, :] = zeros
@@ -336,20 +419,25 @@
     def _():
         stage_y(0)
         stage_y(1)
+        relay_pass(1)
         stage_far(0)
         stage_far(1)
-        pl.when(edge)(lambda: start_y(3, source(3)))
 
     @pl.when(is_one)
     def _():
         stage_z(0)
         stage_z(1)
+        relay_pass(1)
         stage_y(0)
         stage_y(1)
+        pl.when(edge)(lambda: stage_z(3))
         stage_done(0, (1, 2, 3))
         stage_done(1, (1, 2, 3))
 
+    relay_pass(2)
+    relay_pass(3)
     edge_zero, edge_one = jnp.logical_and(edge, is_zero), jnp.logical_and(edge, is_one)
+    sharing = jnp.logical_and(is_one, inner_source_of_two)
 
     def on(flag, n, at, *stages):
         @pl.when(jnp.logical_and(flag, n == at))
@@ -365,7 +453,11 @@
         on(is_zero, n, 3, lambda: stage_x(2))
         on(is_one, n, 0, lambda: stage_far(0))
         on(is_one, n, 1, lambda: stage_far(1))
-        on(edge_one, n, 2, lambda: stage_z(3))
+        on(edge_zero, n, 0, lambda: stage_y(3))
+        on(edge_one, n, 2, lambda: stage_y(3))
+        on(is_zero, n, 2, lambda: start_y(2, source(2)))
+        on(edge_zero, n, 3, lambda: stage_far(3))
+        on(sharing, n, 3, stage_share)
 
     @pl.when(is_zero)
     def _():
@@ -380,13 +472,11 @@
         def _():
             send_hidden(0, chunks - n)
 
-        on(is_zero, n, 0, lambda: start_y(2, source(2)))
-        on(edge_zero, n, 0, lambda: stage_y(3))
         on(is_one, n, 0, lambda: stage_x(0))
         on(is_one, n, 1, lambda: stage_x(3))
-        on(edge_one, n, 1, lambda: stage_y(3))
+        on(edge_one, n, 0, lambda: stage_far(3))
         on(is_one, n, 2, lambda: stage_x(1))
-        on(edge_zero, n, 3, lambda: stage_far(3))
+        on(is_one, n, 3, lambda: stage_z(2))
 
     pl.when(is_one)(lambda: stage_x_done((1, 2, 3)))
 
@@ -399,8 +489,7 @@
             send_hidden(0, 0)
 
         on(is_one, n, 0, lambda: stage_x(2))
-        on(edge_one, n, 1, lambda: stage_far(3))
-        on(is_one, n, 2, lambda: stage_z(2))
+        on(is_zero, n, 2, lambda: stage_y(2))
 
     pl.when(is_zero)(lambda: stage_x_done(range(4)))
 
@@ -412,26 +501,55 @@
         def _():
             send_hidden(1, chunks - n)
 
-        on(is_zero, n, 1, lambda: stage_y(2))
-        on(is_one, n, 2, lambda: stage_y(2))
+        on(is_one, n, 0, lambda: stage_y(2))
 
     stage_far(2)
     send_hidden(1, 0)
 
+    def made_copy(q, i):
+        rows = rows_of(i + FAR_CHUNKS)
+        return remote(
+            made.at[q, :, rows_of(i), :], near.at[far_side, q, :, rows, :], csend.at[q, i], crecv.at[q, i], dp, partner
+        )
+
+    def far_step(n):
+        p, i = n // FAR_CHUNKS, n % FAR_CHUNKS
+        return (x + p) % 2, i
+
     @pl.when(far_any)
     def _():
-        for n in range(FAR_PARTS):
-            far_copy(n).wait()
-        xcat_far[0:breadth, :] = zeros
-        prepare(vid_far, xcat_far, far_rows // breadth)
+        far_upper().wait()
+        far_lower().wait_send()
+        to_relay().wait_send()
+
+    @pl.when(aid_any)
+    def _():
+        far_lower().wait_recv()
+        from_relay(0, partner).wait_recv()
+
+    @pl.when(team)
+    def _():
+        blank = jnp.where(far_any, 0, far_rows)
+        xcat_far[pl.ds(pl.multiple_of(blank, breadth), breadth), :] = zeros
+        prepare(vid_far, xcat_far, far_rows // breadth, one(far_any))
 
         @pl.loop(0, 2 * FAR_CHUNKS)
         def _(n):
             p, i = n // FAR_CHUNKS, n % FAR_CHUNKS
             pair = ((x + p) % 4, (x + p + 2) % 4)
             hidden = activate(half_dot(xcat_far, 0, pair, i) + half_dot(xcat_far, 1, pair, i), pair)
-            for m, j in enumerate(pair):
-                near[far_side, j % 2, j // 2, rows_of(i), :] = hidden[:, m * BLOCK : (m + 1) * BLOCK]
+
+            @pl.when(far_any)
+            def _():
+                for m, j in enumerate(pair):
+                    near[far_side, j % 2, j // 2, rows_of(i), :] = hidden[:, m * BLOCK : (m + 1) * BLOCK]
+
+            @pl.when(aid_any)
+            def _():
+                for m, j in enumerate(pair):
+                    made[j % 2, j // 2, rows_of(i), :] = hidden[:, m * BLOCK : (m + 1) * BLOCK]
+
+            pl.when(jnp.logical_and(aid_any, n > 0))(lambda: made_copy(*far_step(n - 1)).start())
 
     pl.when(is_zero)(lambda: stage_done(2, range(4)))
     pl.when(is_one)(lambda: stage_done(2, (1, 2, 3)))
@@ -448,9 +566,16 @@
     def _(n):
         acc[rows_of(n), :] = temporal(1, own, 0, n) + temporal(1, own, 1, n) + tb_ref[...]
 
+    pl.when(aid_any)(lambda: made_copy(*far_step(2 * FAR_CHUNKS - 1)).start())
     wait_sends()
 
-    x_before, x_after = (t + tiles - 1) % tiles // 8, (t + 1) % tiles // 8
+    @pl.when(is_relay)
+    def _():
+        for n in range(FLOWS):
+            from_relay(n, partner).wait_send()
+
+    x_before = jnp.where(far_before, x, (t + tiles - 1) % tiles // 8)
+    x_after = jnp.where(far_after, x, (t + 1) % tiles // 8)
     for p in range(2):
         @pl.loop(0, chunks)
         def _(n, p=p):
@@ -458,7 +583,9 @@
             rows = rows_of(i)
             for side, there, x_there in ((0, has_before, x_before), (1, has_after, x_after)):
                 q = (x_there + p) % 2
-                pl.when(exchanged(side, i))(lambda: hcopy(q, i, 1 - side).wait_recv())
+                pl.when(exchanged(side))(lambda: hcopy(q, i, 1 - side).wait_recv())
+                from_aid = jnp.logical_and((far_before, far_after)[side], i >= FAR_CHUNKS)
+                pl.when(from_aid)(lambda: made_copy(q, i - FAR_CHUNKS).wait_recv())
 
                 @pl.when(there)
                 def _():
@@ -470,10 +597,16 @@
     @pl.loop(0, chunks)
     def _(i):
         for side in range(2):
-            @pl.when(exchanged(side, i))
+            @pl.when(exchanged(side))
             def _():
                 for q in range(2):
                     hcopy(q, i, side).wait_send()
+
+    @pl.when(aid_any)
+    def _():
+        for q in range(2):
+            for i in range(FAR_CHUNKS):
+                made_copy(q, i).wait_send()
 
 
 def per_device(videos, spatial_filter, temporal_filter, spatial_bias, temporal_bias):
@@ -496,6 +629,8 @@
             pltpu.VMEM((pixels + 2 * breadth, 3 * chans), bf),
             pltpu.VMEM((far_pixels + breadth, 3 * chans), bf),
             pltpu.VMEM((far_pixels, chans), bf),
+            pltpu.VMEM((FLOWS, RELAYED * breadth, chans), bf),
+            pltpu.VMEM((2, blocks // 2, FAR_CHUNKS * ROWS, BLOCK), bf),
             pltpu.VMEM((blocks, 2, TAPS_S, chans // 2, BLOCK), bf),
             pltpu.VMEM((TAPS_T, chans, chans), bf),
             pltpu.VMEM((2, blocks // 2, pixels, BLOCK), bf),
@@ -504,11 +639,13 @@
             pltpu.VMEM((blocks, 1, BLOCK), jnp.float32),
             pltpu.VMEM((1, chans), jnp.float32),
             dma((8,)),
-            dma((4, 10)), dma((4, 9)),
+            dma((4, 11)), dma((4, 9)),
             dma((2, 4)), dma((2, 4)),
             dma((2, 4)), dma((2, 4)),
             dma((2, 2 * chunks)), dma((2, 2 * chunks)),
-            dma((2, FAR_PARTS)),
+            dma((2, 3)),
+            dma((2, FLOWS)),
+            dma((2, FAR_CHUNKS)), dma((2, FAR_CHUNKS)),
         ],
         compiler_params=pltpu.CompilerParams(
             collective_id=0, has_side_effects=True, vmem_limit_bytes=56 * 1024 * 1024

time: 67 us -> 60.5 us (0.903)
  the two profiles are of different devices: /device:TPU:34 before, /device:TPU:1 now
where the time goes in v6:
time: 60.5 us; the launch traced here: 60.4 us
  Pallas kernels  59 us (98%)
  local copies, waits for them, and re-layouts  1.32 us (2%)
    pallas_call x1, Pallas kernels, per_device(): pl.pallas_call(functools.partial(kernel, (height, breadth, chans, shard))...  59 us
    unnamed x1, local copies, waits for them, and re-layouts  1.32 us

profile of v6, /device:TPU:1, one launch (start us, length us, event | category | flops | bytes accessed | tf_op | source)
XLA Modules:
  0.0 60.4 jit_solution(12411695442757183415)
XLA Ops:
  0.0 59.0 %shard_map.55 = bf16[2048,512]{1,0:T(8,128)(2,1)S(1)} custom-call(bf16[2048,512]{1,0:T(8,128)(2,1)} %bitcast.5, bf16[9,64,512]{2,1,0:T(8,128)(2,1)} %ws_hbm.1, bf16[3,64,512]{2,1,0:T(8,128)(2,1)} %wt_hbm.1, f32[4,1,128]{2,1,0:T(1,128)} %bitcast.6, f32[1,512]{1,0:T(1,128)} %bitcast.7), custom_call_target="tpu_custom_call" | custom-call | tf_op jit(solution)/shard_map/pallas_call | solution.py:623
  59.0 1.3 %copy.7 = bf16[1,1,32,64,512]{4,3,2,1,0:T(8,128)(2,1)} copy(bf16[1,1,32,64,512]{4,3,2,1,0:T(8,128)(2,1)S(1)} %bitcast.4) | data formatting | bytes 4194304

commit v7 on v6

--- a/solution.py
+++ b/solution.py
@@ -10,7 +10,7 @@
 BLOCK = 128
 ROWS = 512
 FAR_CHUNKS = 2
-RELAYED = 3
+RELAYED = 4
 FLOWS = 3
 TAPS_S, TAPS_T = 9, 3
 MESH = pl.DeviceIdType.MESH
@@ -299,7 +299,7 @@
         slot = q * chunks + i
         return remote(
             own.at[q, :, rows_of(i), :], near.at[1 - side, q, :, rows_of(i), :],
-            hsend.at[side, slot], hrecv.at[side, slot], dp, t - 1 if side == 0 else t + 1,
+            hsend.at[side], hrecv.at[side, slot], dp, t - 1 if side == 0 else t + 1,
         )
 
     def exchanged(side):
@@ -311,17 +311,25 @@
             pl.when(exchanged(side))(lambda: hcopy((x + p) % 2, i, side).start())
 
     far_rows = (FAR_CHUNKS * ROWS // breadth + 1) * breadth
-    low_from = pixels - far_rows
-    kept = far_rows - RELAYED * breadth
-    passed = pl.ds(low_from + kept, RELAYED * breadth)
+    half_rows = far_rows - breadth
+    kept = half_rows - RELAYED * breadth
+    passed = pl.ds(half_rows + kept, RELAYED * breadth)
 
     def far_upper():
-        rows = pl.ds(0, far_rows)
+        rows = pl.ds(0, half_rows)
         return remote(vid_hbm.at[rows], vid_far.at[rows], vsem.at[0, 0], vsem.at[1, 0], dp, far_tile)
 
     def far_lower():
         return remote(
-            vid_hbm.at[pl.ds(low_from, kept)], vid_far.at[pl.ds(0, kept)], vsem.at[0, 1], vsem.at[1, 1], dp, two_off
+            vid_hbm.at[pl.ds(half_rows, kept)], vid_far.at[pl.ds(breadth, kept)],
+            vsem.at[0, 1], vsem.at[1, 1], dp, two_off,
+        )
+
+    def hand_row():
+        src = pl.multiple_of(jnp.where(far_any, half_rows - breadth, breadth), breadth)
+        dst = pl.multiple_of(jnp.where(far_any, 0, half_rows), breadth)
+        return remote(
+            vid_far.at[pl.ds(src, breadth)], vid_far.at[pl.ds(dst, breadth)], vsem.at[0, 3], vsem.at[1, 3], dp, partner
         )
 
     def to_relay():
@@ -329,7 +337,7 @@
 
     def from_relay(n, to_tile):
         return remote(
-            relayed.at[n], vid_far.at[pl.ds(kept, RELAYED * breadth)], rsem.at[1, n], vsem.at[1, 2], dp, to_tile
+            relayed.at[n], vid_far.at[pl.ds(breadth + kept, RELAYED * breadth)], rsem.at[1, n], vsem.at[1, 2], dp, to_tile
         )
 
     def relay_pass(distance):
@@ -501,6 +509,8 @@
         def _():
             send_hidden(1, chunks - n)
 
+        on(far_any, n, 1, lambda: far_upper().wait_recv(), lambda: hand_row().start())
+        on(aid_any, n, 0, lambda: far_lower().wait_recv(), lambda: hand_row().start())
         on(is_one, n, 0, lambda: stage_y(2))
 
     stage_far(2)
@@ -518,17 +528,17 @@
 
     @pl.when(far_any)
     def _():
-        far_upper().wait()
+        far_upper().wait_send()
         far_lower().wait_send()
         to_relay().wait_send()
 
     @pl.when(aid_any)
     def _():
-        far_lower().wait_recv()
         from_relay(0, partner).wait_recv()
 
     @pl.when(team)
     def _():
+        hand_row().wait()
         blank = jnp.where(far_any, 0, far_rows)
         xcat_far[pl.ds(pl.multiple_of(blank, breadth), breadth), :] = zeros
         prepare(vid_far, xcat_far, far_rows // breadth, one(far_any))
@@ -562,9 +572,11 @@
         rhs = jnp.concatenate([taps(lag, q), taps(lag, q + 2)], axis=0)
         return jnp.dot(lhs, rhs, preferred_element_type=jnp.float32)
 
-    @pl.loop(0, chunks)
-    def _(n):
-        acc[rows_of(n), :] = temporal(1, own, 0, n) + temporal(1, own, 1, n) + tb_ref[...]
+    @pl.when(jnp.logical_not(team))
+    def _():
+        @pl.loop(0, chunks)
+        def _(n):
+            acc[rows_of(n), :] = temporal(1, own, 0, n) + temporal(1, own, 1, n) + tb_ref[...]
 
     pl.when(aid_any)(lambda: made_copy(*far_step(2 * FAR_CHUNKS - 1)).start())
     wait_sends()
@@ -574,33 +586,82 @@
         for n in range(FLOWS):
             from_relay(n, partner).wait_send()
 
-    x_before = jnp.where(far_before, x, (t + tiles - 1) % tiles // 8)
-    x_after = jnp.where(far_after, x, (t + 1) % tiles // 8)
-    for p in range(2):
+    there, x_there = (has_before, has_after), ((t + tiles - 1) % tiles // 8, (t + 1) % tiles // 8)
+
+    @pl.when(jnp.logical_not(team))
+    def _():
+        for p in range(2):
+            @pl.loop(0, chunks)
+            def _(n, p=p):
+                i = chunks - 1 - n
+                rows = rows_of(i)
+                for side in range(2):
+                    @pl.when(there[side])
+                    def _():
+                        q = (x_there[side] + p) % 2
+                        hcopy(q, i, 1 - side).wait_recv()
+                        acc[rows, :] += temporal(2 * side, near.at[side], q, i)
+
+                if p == 1:
+                    outv[rows, :] = acc[rows, :].astype(jnp.bfloat16)
+
+    @pl.when(aid_any)
+    def _():
+        z_side = jnp.where(aid_before, 1, 0)
+        q_first = jnp.where(aid_before, x_there[1], x_there[0]) % 2
+
         @pl.loop(0, chunks)
-        def _(n, p=p):
+        def _(n):
             i = chunks - 1 - n
-            rows = rows_of(i)
-            for side, there, x_there in ((0, has_before, x_before), (1, has_after, x_after)):
-                q = (x_there + p) % 2
-                pl.when(exchanged(side))(lambda: hcopy(q, i, 1 - side).wait_recv())
-                from_aid = jnp.logical_and((far_before, far_after)[side], i >= FAR_CHUNKS)
-                pl.when(from_aid)(lambda: made_copy(q, i - FAR_CHUNKS).wait_recv())
-
-                @pl.when(there)
-                def _():
-                    acc[rows, :] += temporal(2 * side, near.at[side], q, i)
-
-            if p == 1:
-                outv[rows, :] = acc[rows, :].astype(jnp.bfloat16)
-
-    @pl.loop(0, chunks)
-    def _(i):
-        for side in range(2):
-            @pl.when(exchanged(side))
+
+            @pl.when(aid_before)
+            def _():
+                hcopy(q_first, i, 0).wait_recv()
+                for q in range(2):
+                    hcopy(q, i, 1).wait_recv()
+
+            @pl.when(aid_after)
+            def _():
+                hcopy(q_first, i, 1).wait_recv()
+                for q in range(2):
+                    hcopy(q, i, 0).wait_recv()
+
+            total = tb_ref[...] + temporal(2 * z_side, near.at[z_side], q_first, i)
+            for q in range(2):
+                total = total + temporal(1, own, q, i) + temporal(2 - 2 * z_side, near.at[1 - z_side], q, i)
+            acc[rows_of(i), :] = total
+
+        @pl.loop(0, chunks)
+        def _(n):
+            i = chunks - 1 - n
+            pl.when(aid_before)(lambda: hcopy(1 - q_first, i, 0).wait_recv())
+            pl.when(aid_after)(lambda: hcopy(1 - q_first, i, 1).wait_recv())
+            rest = temporal(2 * z_side, near.at[z_side], 1 - q_first, i)
+            outv[rows_of(i), :] = (acc[rows_of(i), :] + rest).astype(jnp.bfloat16)
+
+    @pl.when(far_any)
+    def _():
+        @pl.loop(0, chunks)
+        def _(i):
+            pl.when(far_before)(lambda: [hcopy(q, i, 0).wait_recv() for q in range(2)] and None)
+            pl.when(far_after)(lambda: [hcopy(q, i, 1).wait_recv() for q in range(2)] and None)
+
+            @pl.when(i >= FAR_CHUNKS)
             def _():
                 for q in range(2):
-                    hcopy(q, i, side).wait_send()
+                    made_copy(q, i - FAR_CHUNKS).wait_recv()
+
+            total = tb_ref[...]
+            for q in range(2):
+                total = total + temporal(1, own, q, i)
+                for side in range(2):
+                    total = total + temporal(2 * side, near.at[side], q, i)
+            outv[rows_of(i), :] = total.astype(jnp.bfloat16)
+
+    for side in range(2):
+        @pl.when(exchanged(side))
+        def _():
+            remote(own, near.at[1 - side], hsend.at[side], hrecv.at[side, 0], dp, partner).wait_send()
 
     @pl.when(aid_any)
     def _():
@@ -642,8 +703,8 @@
             dma((4, 11)), dma((4, 9)),
             dma((2, 4)), dma((2, 4)),
             dma((2, 4)), dma((2, 4)),
-            dma((2, 2 * chunks)), dma((2, 2 * chunks)),
-            dma((2, 3)),
+            dma((2,)), dma((2, 2 * chunks)),
+            dma((2, 4)),
             dma((2, FLOWS)),
             dma((2, FAR_CHUNKS)), dma((2, FAR_CHUNKS)),
         ],

time: 60.5 us -> 58.4 us (0.965)
  the two profiles are of different devices: /device:TPU:1 before, /device:TPU:34 now
where the time goes in v7:
time: 58.4 us; the launch traced here: 58 us
  Pallas kernels  56.6 us (97%)
  local copies, waits for them, and re-layouts  1.32 us (2%)
    pallas_call x1, Pallas kernels, per_device(): pl.pallas_call(functools.partial(kernel, (height, breadth, chans, shard))...  56.6 us
    unnamed x1, local copies, waits for them, and re-layouts  1.32 us

profile of v7, /device:TPU:34, one launch (start us, length us, event | category | flops | bytes accessed | tf_op | source)
XLA Modules:
  0.0 58.0 jit_solution(6487351674343157018)
XLA Ops:
  0.0 56.6 %shard_map.55 = bf16[2048,512]{1,0:T(8,128)(2,1)S(1)} custom-call(bf16[2048,512]{1,0:T(8,128)(2,1)} %bitcast.5, bf16[9,64,512]{2,1,0:T(8,128)(2,1)} %ws_hbm.1, bf16[3,64,512]{2,1,0:T(8,128)(2,1)} %wt_hbm.1, f32[4,1,128]{2,1,0:T(1,128)} %bitcast.6, f32[1,512]{1,0:T(1,128)} %bitcast.7), custom_call_target="tpu_custom_call" | custom-call | tf_op jit(solution)/shard_map/pallas_call | solution.py:684
  56.6 1.3 %copy.7 = bf16[1,1,32,64,512]{4,3,2,1,0:T(8,128)(2,1)} copy(bf16[1,1,32,64,512]{4,3,2,1,0:T(8,128)(2,1)S(1)} %bitcast.4) | data formatting | bytes 4194304

commit v8 on v7

--- a/solution.py
+++ b/solution.py
@@ -156,9 +156,12 @@
         ref = piece(g, y_at, z_at, low, count)
         return remote(ref if src is None else src, ref, wsend.at[g, send], wrecv.at[g, recv], to_dp, to_tile)
 
+    def ring_many(g, send, recv, count):
+        return ring(g, send, recv, 0, 0, dp, partner, 0, count * shard)
+
     def from_x(n, k, y_at, to_tile):
         ref = block_piece(block_a, y_at, carried)
-        return remote(ref, ref, xsend.at[n, k], xrecv.at[n, k], dp, to_tile)
+        return remote(ref, ref, xsend.at[n], xrecv.at[n, k], dp, to_tile)
 
     by_x = jnp.logical_not(first), jnp.logical_not(last)
 
@@ -166,7 +169,7 @@
         return (y + k) % 4
 
     def spread(g, k):
-        ring(g, 6 + k, 5 + k, y_of(k), carried, dp, partner).start()
+        ring(g, 3, 4, y_of(k), carried, dp, partner).start()
         if g == 0:
             pl.when(by_x[0])(lambda: from_x(0, k, y_of(k), x_next).start())
             pl.when(by_x[1])(lambda: from_x(1, k, y_of(k), x_prev).start())
@@ -190,7 +193,7 @@
 
     def start_y(g, src=None):
         ring(g, 2, 1, y, carried, up, t, src=src).start()
-        ring(g, 3, 2, y, carried, dn, t, src=src).start()
+        ring(g, 2, 2, y, carried, dn, t, src=src).start()
 
     inner_source_of_two = jnp.logical_and(jnp.logical_not(edge), in_free)
 
@@ -199,7 +202,7 @@
 
     def stage_share():
         ring(2, 0, 0, y, 1 - zh, dp, partner).wait_recv()
-        for slot, to_tile in ((0, x_next), (1, x_prev), (10, x_across)):
+        for slot, to_tile in ((0, x_next), (0, x_prev), (0, x_across)):
             share(slot, to_tile).start()
 
     def stage_z(g):
@@ -213,53 +216,50 @@
 
     def stage_y(g):
         ring(g, 2, 1, y_of(3), carried, up, t).wait_recv()
-        ring(g, 4, 3, y_of(3), carried, up, t, 0, half).start()
-        ring(g, 3, 2, y_of(1), carried, dn, t).wait_recv()
-        ring(g, 5, 4, y_of(1), carried, dn, t, half, half).start()
+        ring(g, 2, 3, y_of(3), carried, up, t, 0, half).start()
+        ring(g, 2, 2, y_of(1), carried, dn, t).wait_recv()
+        ring(g, 2, 3, y_of(1), carried, dn, t, half, half).start()
         spread(g, 3)
         spread(g, 1)
 
     def stage_far(g):
-        ring(g, 4, 3, y_of(2), carried, up, t, 0, half).wait_recv()
-        ring(g, 5, 4, y_of(2), carried, dn, t, half, half).wait_recv()
+        ring(g, 2, 3, y_of(2), carried, up, t).wait_recv()
         spread(g, 2)
 
     def stage_done(g, ks):
-        for k in ks:
-            ring(g, 6 + k, 5 + k, y_of(k), 1 - carried, dp, partner).wait_recv()
+        ring_many(g, 3, 4, len(ks)).wait_recv()
 
     def onward(n, k, z_at):
         ref = block_piece((block_d, block_c)[n], y_of(k), z_at)
-        return remote(ref, ref, psend.at[n, k], precv.at[n, k], dp, partner)
+        return remote(ref, ref, psend.at[n], precv.at[n], dp, partner)
+
+    def many(n, count, send, recv):
+        ref = block_piece(0, 0, 0, 0, count * shard)
+        return remote(ref, ref, send.at[n], recv, dp, partner)
 
     def stage_x(k):
         for n in range(2):
             @pl.when(by_x[n])
             def _():
                 ref = block_piece((block_d, block_c)[n], y_of(k), carried)
-                remote(ref, ref, xsend.at[n, k], xrecv.at[n, k], dp, x_next).wait_recv()
+                remote(ref, ref, xsend.at[n], xrecv.at[n, k], dp, x_next).wait_recv()
                 onward(n, k, carried).start()
 
     def stage_x_done(ks):
         for n in range(2):
             @pl.when(by_x[n])
             def _():
-                for k in ks:
-                    onward(n, k, 1 - carried).wait_recv()
+                many(n, len(ks), psend, precv.at[n]).wait_recv()
 
         pl.when(edge)(lambda: stage_done(3, ks))
 
+    def by_core(wait):
+        pl.when(is_zero)(lambda: wait(3))
+        pl.when(is_one)(lambda: wait(4))
+
     def wait_ring(g):
-        for slot in (2, 3):
-            ring(g, slot, 0, y, carried, up, t).wait_send()
-        for slot in (4, 5):
-            ring(g, slot, 0, y, carried, up, t, 0, half).wait_send()
-        for k in range(1, 4):
-            ring(g, 6 + k, 5 + k, y, carried, dp, partner).wait_send()
-
-        @pl.when(is_one)
-        def _():
-            ring(g, 6, 5, y, carried, dp, partner).wait_send()
+        ring_many(g, 2, 0, 3).wait_send()
+        by_core(lambda count: ring_many(g, 3, 0, count).wait_send())
 
     def wait_sends():
         for g in range(3):
@@ -277,20 +277,13 @@
 
         @pl.when(jnp.logical_and(is_one, inner_source_of_two))
         def _():
-            for slot in (0, 1, 10):
-                share(slot, x_next).wait_send()
-
-        def wait_x(n, k):
-            from_x(n, k, y, x_next).wait_send()
-            onward(n, k, carried).wait_send()
+            ring_many(2, 0, 0, 3).wait_send()
 
         for n in range(2):
             @pl.when(by_x[n])
             def _():
-                for k in range(1, 4):
-                    wait_x(n, k)
-
-            pl.when(jnp.logical_and(by_x[n], is_one))(lambda: wait_x(n, 0))
+                by_core(lambda count: many(n, count, xsend, xrecv.at[n, 0]).wait_send())
+                by_core(lambda count: many(n, count, psend, precv.at[n]).wait_send())
 
     def rows_of(i):
         return pl.ds(pl.multiple_of(i * ROWS, ROWS), ROWS)
@@ -519,7 +512,7 @@
     def made_copy(q, i):
         rows = rows_of(i + FAR_CHUNKS)
         return remote(
-            made.at[q, :, rows_of(i), :], near.at[far_side, q, :, rows, :], csend.at[q, i], crecv.at[q, i], dp, partner
+            made.at[q, :, rows_of(i), :], near.at[far_side, q, :, rows, :], csend.at[0], crecv.at[i], dp, partner
         )
 
     def far_step(n):
@@ -588,22 +581,33 @@
 
     there, x_there = (has_before, has_after), ((t + tiles - 1) % tiles // 8, (t + 1) % tiles // 8)
 
-    @pl.when(jnp.logical_not(team))
-    def _():
+    def exchange_rest(chip, z):
         for p in range(2):
             @pl.loop(0, chunks)
             def _(n, p=p):
                 i = chunks - 1 - n
                 rows = rows_of(i)
-                for side in range(2):
-                    @pl.when(there[side])
+                q = (x_there[chip] + p) % 2
+                hcopy(q, i, 1 - chip).wait_recv()
+                acc[rows, :] += temporal(2 * chip, near.at[chip], q, i)
+
+                @pl.when(there[z])
+                def _():
+                    q = (x_there[z] + p) % 2
+                    hcopy(q, i, 1 - z).wait_recv()
+                    total = acc[rows, :] + temporal(2 * z, near.at[z], q, i)
+                    if p == 0:
+                        acc[rows, :] = total
+                    else:
+                        outv[rows, :] = total.astype(jnp.bfloat16)
+
+                if p == 1:
+                    @pl.when(jnp.logical_not(there[z]))
                     def _():
-                        q = (x_there[side] + p) % 2
-                        hcopy(q, i, 1 - side).wait_recv()
-                        acc[rows, :] += temporal(2 * side, near.at[side], q, i)
-
-                if p == 1:
-                    outv[rows, :] = acc[rows, :].astype(jnp.bfloat16)
+                        outv[rows, :] = acc[rows, :].astype(jnp.bfloat16)
+
+    pl.when(jnp.logical_and(jnp.logical_not(team), is_zero))(lambda: exchange_rest(1, 0))
+    pl.when(jnp.logical_and(jnp.logical_not(team), is_one))(lambda: exchange_rest(0, 1))
 
     @pl.when(aid_any)
     def _():
@@ -648,8 +652,8 @@
 
             @pl.when(i >= FAR_CHUNKS)
             def _():
-                for q in range(2):
-                    made_copy(q, i - FAR_CHUNKS).wait_recv()
+                both = made.at[:, :, rows_of(i - FAR_CHUNKS), :]
+                remote(both, both, csend.at[0], crecv.at[i - FAR_CHUNKS], dp, partner).wait_recv()
 
             total = tb_ref[...]
             for q in range(2):
@@ -665,9 +669,7 @@
 
     @pl.when(aid_any)
     def _():
-        for q in range(2):
-            for i in range(FAR_CHUNKS):
-                made_copy(q, i).wait_send()
+        remote(made, made, csend.at[0], crecv.at[0], dp, partner).wait_send()
 
 
 def per_device(videos, spatial_filter, temporal_filter, spatial_bias, temporal_bias):
@@ -700,13 +702,13 @@
             pltpu.VMEM((blocks, 1, BLOCK), jnp.float32),
             pltpu.VMEM((1, chans), jnp.float32),
             dma((8,)),
-            dma((4, 11)), dma((4, 9)),
-            dma((2, 4)), dma((2, 4)),
-            dma((2, 4)), dma((2, 4)),
+            dma((4, 4)), dma((4, 5)),
+            dma((2,)), dma((2, 4)),
+            dma((2,)), dma((2,)),
             dma((2,)), dma((2, 2 * chunks)),
             dma((2, 4)),
             dma((2, FLOWS)),
-            dma((2, FAR_CHUNKS)), dma((2, FAR_CHUNKS)),
+            dma((1,)), dma((FAR_CHUNKS,)),
         ],
         compiler_params=pltpu.CompilerParams(
             collective_id=0, has_side_effects=True, vmem_limit_bytes=56 * 1024 * 1024

time: 58.4 us -> 57.6 us (0.986)
  Pallas kernels: 56.6 us -> 55.7 us
    pallas_call x1, Pallas kernels: 56.6 us -> 55.7 us  [per_device(): pl.pallas_call(functools.partial(kernel, (height, breadth, chans, shard))...]
where the time goes in v8:
time: 57.6 us; the launch traced here: 57 us
  Pallas kernels  55.7 us (97%)
  local copies, waits for them, and re-layouts  1.32 us (2%)
    pallas_call x1, Pallas kernels, per_device(): pl.pallas_call(functools.partial(kernel, (height, breadth, chans, shard))...  55.7 us
    unnamed x1, local copies, waits for them, and re-layouts  1.32 us

profile of v8, /device:TPU:34, one launch (start us, length us, event | category | flops | bytes accessed | tf_op | source)
XLA Modules:
  0.0 57.0 jit_solution(1073407649245920691)
XLA Ops:
  0.0 55.7 %shard_map.55 = bf16[2048,512]{1,0:T(8,128)(2,1)S(1)} custom-call(bf16[2048,512]{1,0:T(8,128)(2,1)} %bitcast.5, bf16[9,64,512]{2,1,0:T(8,128)(2,1)} %ws_hbm.1, bf16[3,64,512]{2,1,0:T(8,128)(2,1)} %wt_hbm.1, f32[4,1,128]{2,1,0:T(1,128)} %bitcast.6, f32[1,512]{1,0:T(1,128)} %bitcast.7), custom_call_target="tpu_custom_call" | custom-call | tf_op jit(solution)/shard_map/pallas_call | solution.py:686
  55.7 1.3 %copy.7 = bf16[1,1,32,64,512]{4,3,2,1,0:T(8,128)(2,1)} copy(bf16[1,1,32,64,512]{4,3,2,1,0:T(8,128)(2,1)S(1)} %bitcast.4) | data formatting | bytes 4194304

commit v9 on v8

--- a/solution.py
+++ b/solution.py
@@ -292,7 +292,8 @@
         slot = q * chunks + i
         return remote(
             own.at[q, :, rows_of(i), :], near.at[1 - side, q, :, rows_of(i), :],
-            hsend.at[side], hrecv.at[side, slot], dp, t - 1 if side == 0 else t + 1,
+            hsend.at[side], hrecv.at[side, slot], dp,
+            jnp.maximum(t - 1, 0) if side == 0 else jnp.minimum(t + 1, tiles - 1),
         )
 
     def exchanged(side):

time: 57.6 us -> 57.6 us (level)
  no operation moved by 1% of the time
where the time goes in v9:
time: 57.6 us; the launch traced here: 57 us
  Pallas kernels  55.7 us (97%)
  local copies, waits for them, and re-layouts  1.32 us (2%)
    pallas_call x1, Pallas kernels, per_device(): pl.pallas_call(functools.partial(kernel, (height, breadth, chans, shard))...  55.7 us
    unnamed x1, local copies, waits for them, and re-layouts  1.32 us

profile of v9, /device:TPU:34, one launch (start us, length us, event | category | flops | bytes accessed | tf_op | source)
XLA Modules:
  0.0 57.0 jit_solution(10074843701537187459)
XLA Ops:
  0.0 55.7 %shard_map.55 = bf16[2048,512]{1,0:T(8,128)(2,1)S(1)} custom-call(bf16[2048,512]{1,0:T(8,128)(2,1)} %bitcast.5, bf16[9,64,512]{2,1,0:T(8,128)(2,1)} %ws_hbm.1, bf16[3,64,512]{2,1,0:T(8,128)(2,1)} %wt_hbm.1, f32[4,1,128]{2,1,0:T(1,128)} %bitcast.6, f32[1,512]{1,0:T(1,128)} %bitcast.7), custom_call_target="tpu_custom_call" | custom-call | tf_op jit(solution)/shard_map/pallas_call | solution.py:687
  55.7 1.3 %copy.7 = bf16[1,1,32,64,512]{4,3,2,1,0:T(8,128)(2,1)} copy(bf16[1,1,32,64,512]{4,3,2,1,0:T(8,128)(2,1)S(1)} %bitcast.4) | data formatting | bytes 4194304

commit v10 on v9

--- a/solution.py
+++ b/solution.py
@@ -98,9 +98,6 @@
     loads.append(pltpu.make_async_copy(wt_hbm, piece(2, y, zh), local_sem.at[4]))
     loads.append(pltpu.make_async_copy(sb_hbm, sb_ref, local_sem.at[6]))
     loads.append(pltpu.make_async_copy(tb_hbm, tb_ref, local_sem.at[7]))
-    vid_copy.start()
-    for load in loads:
-        load.start()
 
     barrier = pltpu.get_barrier_semaphore()
 
@@ -148,6 +145,10 @@
     @pl.when(has_after)
     def _():
         greet(dp, t + 1)
+
+    vid_copy.start()
+    for load in loads:
+        load.start()
 
     one = lambda flag: jnp.where(flag, 1, 0)
     pl.semaphore_wait(barrier, 7 + one(edge) + one(has_before) + one(has_after) + 2 * one(team) + 2 * FLOWS * one(is_relay))

time: 57.6 us -> 57.5 us (level)
  no operation moved by 1% of the time
where the time goes in v10:
time: 57.5 us; the launch traced here: 57 us
  Pallas kernels  55.6 us (97%)
  local copies, waits for them, and re-layouts  1.32 us (2%)
    pallas_call x1, Pallas kernels, per_device(): pl.pallas_call(functools.partial(kernel, (height, breadth, chans, shard))...  55.6 us
    unnamed x1, local copies, waits for them, and re-layouts  1.32 us

profile of v10, /device:TPU:34, one launch (start us, length us, event | category | flops | bytes accessed | tf_op | source)
XLA Modules:
  0.0 57.0 jit_solution(11256252547970334708)
XLA Ops:
  0.0 55.6 %shard_map.55 = bf16[2048,512]{1,0:T(8,128)(2,1)S(1)} custom-call(bf16[2048,512]{1,0:T(8,128)(2,1)} %bitcast.5, bf16[9,64,512]{2,1,0:T(8,128)(2,1)} %ws_hbm.1, bf16[3,64,512]{2,1,0:T(8,128)(2,1)} %wt_hbm.1, f32[4,1,128]{2,1,0:T(1,128)} %bitcast.6, f32[1,512]{1,0:T(1,128)} %bitcast.7), custom_call_target="tpu_custom_call" | custom-call | tf_op jit(solution)/shard_map/pallas_call | solution.py:688
  55.7 1.3 %copy.7 = bf16[1,1,32,64,512]{4,3,2,1,0:T(8,128)(2,1)} copy(bf16[1,1,32,64,512]{4,3,2,1,0:T(8,128)(2,1)S(1)} %bitcast.4) | data formatting | bytes 4194304
